TPU v7x, 32 devices: a whole 2x2x4 slice. The times are simulated.
32 devices in a mesh: real: 2 (over x), bx: 4 (over y, core), by: 4 (over z).
Axes of the slice: x: 2, y: 2, z: 4, core: 2. Of those that a mesh axis runs over, the one named last changes fastest.
Arguments:
- current: float32 [2, 12, 3, 8, 32, 128], P('real', None, None, 'bx', 'by'), may hold values from -110 to 110
- previous: float32 [2, 12, 3, 8, 32, 128], P('real', None, None, 'bx', 'by'), may hold values from -110 to 110
- element_stiffness: float32 [24, 24], replicated, may hold values from -0.75 to 1.25, as said below
- preconditioner: float32 [2, 3, 8, 32, 128], P('real', None, 'bx', 'by'), may hold values from 0.04 to 0.16
- modulus: float32 [8, 32, 128], P('bx', 'by'), may hold values from 0.3 to 9.1
- density: float32 [8, 32, 128], P('bx', 'by'), may hold values from 0.5 to 2
- solid: int32 [2, 8, 32, 128], P('real', 'bx', 'by'), may hold values from 0 to 1, as said below
- clamped: int32 [8, 32], P('bx', 'by'), may hold values 0 or 1
Outputs:
- gram_stiff: float32 [2, 36, 36], P('real')
- gram_mass: float32 [2, 36, 36], P('real')
- search_block: float32 [2, 12, 3, 8, 32, 128], P('real', None, None, 'bx', 'by')
- sensitivity: float32 [8, 32, 128], P('bx', 'by', 'real')
Inputs may be any that keep to these rules, and one draw needn't show every extreme that they name: `element_stiffness`: symmetric positive definite: the stiffness of a trilinear brick of unit edge for unit modulus and a Poisson ratio between 0.25 and 0.35, divided by its diagonal entry, plus a small positive definite part. 1 marks a solid element of that realization; a realization's solid elements include those of every realization before it. `clamped`: 1 marks a bottom-face node held in all three directions.
All inputs are finite; a program needn't handle non-finite values. No bound on the sum of `clamped` on one device may be relied on, other than what follows from the above.
Results may differ from a plain program's by a relative error of at most 0.00013.
Values sent between devices are 32-bit elements; how exact they have to be, the bound alone decides.
No kernel may reach another device: no remote copies, remote signals or barrier semaphores. Data moves between devices by JAX's collectives and lax.ppermute only.
A program may use at most 64 MiB of HBM per device.

v0:
```python
import numpy as np
import jax
import jax.numpy as jnp
from jax import lax
from jax.experimental import pallas as pl
from jax.experimental.pallas import tpu as pltpu
from jax.sharding import PartitionSpec as P

f32 = jnp.float32
bf16 = jnp.bfloat16
SLAB = 16
NODE_ROWS = 112
FORCE_ROWS = 192
OTHER_TOP = 120
EDGE = 64


def operator_tables(rows):
    row_pick = np.zeros((2, NODE_ROWS + FORCE_ROWS, 24), np.float32)
    col_pick = np.zeros((24, FORCE_ROWS + EDGE), np.float32)
    col_y = np.full(FORCE_ROWS + EDGE, -99)
    for beta in range(24):
        for y in range(rows):
            col_pick[beta, beta * rows + y] = 1
            col_y[beta * rows + y] = y
    for a in range(2):
        for q in range(2):
            for d in range(3):
                for j in range(4):
                    k = FORCE_ROWS + (a * 2 + q) * 16 + d * 4 + j
                    col_pick[(4 * a + 2 * (j % 2) + q) * 3 + d, k] = 1
                    col_y[k] = -1 if j < 2 else rows
    mask = np.zeros((2, NODE_ROWS + FORCE_ROWS, FORCE_ROWS + EDGE), np.float32)
    for q in range(2):
        for a in range(2):
            for d in range(3):
                for y in range(rows + 1):
                    m = (q * 6 + a * 3 + d) * rows + y
                    if y == rows:
                        m = 12 * rows + q * 8 + a * 3 + d
                    for b in range(2):
                        row_pick[b, m, (4 * a + 2 * b + q) * 3 + d] = 1
                        mask[b, m] = col_y == y - b
    for alpha in range(24):
        for y in range(rows):
            m = NODE_ROWS + alpha * rows + y
            row_pick[0, m, alpha] = 1
            mask[0, m, :FORCE_ROWS] = col_y[:FORCE_ROWS] == y
    return row_pick, col_pick, mask


def split(value):
    high = value.astype(bf16)
    return high, (value - high.astype(f32)).astype(bf16)


def dot(left, right):
    return jnp.dot(left, right, preferred_element_type=f32)


def fetch(sources, buffers, arrived):
    copies = [pltpu.make_async_copy(source, buffer, arrived.at[i]) for i, (source, buffer) in enumerate(zip(sources, buffers))]
    for copy in copies:
        copy.start()
    for copy in copies:
        copy.wait()
    return buffers


def operator_kernel(*refs):
    high_out, low_out = refs[4:6]
    matrix, row_pick, col_pick, mask = fetch(refs[0:4], refs[6:10], refs[10])
    high, low = split(matrix[...])
    for part, out in ((high, high_out), (low, low_out)):
        total = 0.0
        for b in range(2):
            picked = dot(row_pick[b], part).astype(bf16)
            total = total + dot(picked, col_pick[...]) * mask[b].astype(f32)
        out[...] = total.astype(bf16)


def prepare_kernel(sizes, *refs):
    own, prev_free, up, down = refs[7:11]
    cur, prev, modulus, density, solid, precond, clamped = fetch(refs[0:7], refs[11:18], refs[18])
    cols, sx, sy, sz = sizes
    slabs = cols * 3
    block = slabs * sx * sy
    held = clamped[...].astype(f32)
    eye = (lax.broadcasted_iota(jnp.int32, (sy, sy), 0) == lax.broadcasted_iota(jnp.int32, (sy, sy), 1)).astype(f32)
    bottom = (lax.broadcasted_iota(jnp.int32, (sy, sz), 1) == 0).astype(f32)
    planes = []
    for x in range(sx):
        column = jnp.sum(jnp.broadcast_to(held[x : x + 1], (sy, sy)) * eye, 1, keepdims=True)
        planes.append((1.0 - column * bottom)[None])
    free = jnp.concatenate(planes, 0)
    share = solid[0].astype(f32)
    own[0:block] = (cur[0] * free[None, None]).reshape(block, sz)
    masked = prev[0] * free[None, None]
    prev_free[...] = masked.reshape(block, sz)
    own[block : block + slabs * sy] = masked[:, :, 0].reshape(slabs * sy, sz)
    field = block + slabs * sy
    plane = sx * sy
    own[field : field + plane] = (modulus[...] * (0.02 + 0.98 * share)).reshape(plane, sz)
    own[field + plane : field + 2 * plane] = (density[...] * (0.1 + 0.9 * share) * 0.125).reshape(plane, sz)
    own[field + 2 * plane : field + 5 * plane] = (precond[0] * free[None]).reshape(3 * plane, sz)
    n = slabs * sx
    up[0:n] = own[pl.ds(sy - 1, n, stride=sy), :]
    up[n : n + 2 * sx] = own[pl.ds(field + sy - 1, 2 * sx, stride=sy), :]
    up[n + 2 * sx :] = jnp.zeros((up.shape[0] - n - 2 * sx, sz), f32)
    down[0:n] = own[pl.ds(0, n, stride=sy), :]
    down[n : 2 * n] = own[pl.ds(1, n, stride=sy), :]
    down[2 * n : 3 * n] = prev_free[pl.ds(0, n, stride=sy), :]
    down[3 * n : 3 * n + 5 * sx] = own[pl.ds(field, 5 * sx, stride=sy), :]
    down[3 * n + 5 * sx :] = jnp.zeros((down.shape[0] - 3 * n - 5 * sx, sz), f32)


def helpers(sizes, basis, stiff, op_high, op_low):
    cols, _, sy, sz = sizes
    width = 4 * cols
    span = sy + 1
    lane = lax.broadcasted_iota(jnp.int32, (8, sz), 1)
    not_last = (lane < sz - 1).astype(f32)
    not_first = (lane > 0).astype(f32)

    def base(layer, k, d):
        return (((layer + 1) * width + k) * 3 + d) * span

    def out_base(layer, k, d):
        return ((layer * width + k) * 3 + d) * span

    def corner_tiles(k, layer):
        tiles = []
        for a in range(2):
            for b in range(2):
                near = [basis[pl.ds(base(layer + a, k, d) + b, sy), :] for d in range(3)]
                tiles += near
                tiles += [pltpu.roll(tile, sz - 1, 1) for tile in near]
        return tiles

    def weights(layer):
        plain = stiff[pl.ds((layer + 1) * sy, sy), :]
        return plain, plain * not_last

    def scaled(tiles, layer):
        plain, cut = weights(layer)
        return [tile * (cut if (i // 3) % 2 else plain) for i, tile in enumerate(tiles)]

    def apply(columns, rows, depth):
        value = jnp.concatenate(columns, 1)
        high = value.astype(bf16)
        rest = value - high.astype(f32)
        both = dot(jnp.concatenate([op_high[0:rows, 0:depth], op_low[0:rows, 0:depth]], 0), high)
        total = both[0:rows] + both[rows:]
        nodes = total[0:NODE_ROWS] + dot(op_high[0:NODE_ROWS, 0:depth], rest.astype(bf16))
        return nodes, total[NODE_ROWS:], value[0:FORCE_ROWS] + rest[0:FORCE_ROWS]

    def node_parts(out):
        parts = []
        for i in range(6):
            shifted = pltpu.roll(out[(6 + i) * sy : (7 + i) * sy], 1, 1) * not_first
            parts.append(out[i * sy : (i + 1) * sy] + shifted)
        rim = out[12 * sy : 12 * sy + 8] + pltpu.roll(out[12 * sy + 8 : 12 * sy + 16], 1, 1) * not_first
        return parts, rim

    return base, out_base, not_last, not_first, corner_tiles, weights, scaled, apply, node_parts


def current_kernel(
    sizes, place, own, prev_free, from_low, from_high,
    pair_a, pair_b, corner_a, corner_b, op_high, op_low,
    basis, applied, a_out, b_out, stiff_out, mass_out, share_out, stiff, lumped,
    edge, stiff_edge, mass_rows, scale, above, below,
):
    cols, sx, sy, sz = sizes
    slabs = cols * 3
    block = slabs * sx * sy
    plane = sx * sy
    field = block + slabs * sy
    low_rows = from_low.shape[0]
    n = slabs * sx
    span = sy + 1

    base, out_base, not_last, not_first, corner_tiles, weights, scaled, apply, node_parts = helpers(
        sizes, basis, stiff, op_high, op_low
    )

    def unpack(layer, source, low, high, at):
        low_ref, low_at = low
        high_ref, high_at = high
        for k in range(cols):
            for d in range(3):
                basis[pl.ds(base(layer, k, d), sy), :] = source[pl.ds(((k * 3 + d) * sx + at) * sy, sy), :]
        basis[pl.ds(base(layer, 0, 0) + sy, slabs, stride=span), :] = high_ref[pl.ds(high_at + at, slabs, stride=sx), :]
        for d in range(3):
            start = (layer + 1) * cols * SLAB + d * 4
            pick = d * sx + at
            edge[pl.ds(start, cols, stride=SLAB), :] = low_ref[pl.ds(low_at + pick, cols, stride=3 * sx), :]
            edge[pl.ds(start + 1, cols, stride=SLAB), :] = source[pl.ds(pick * sy, cols, stride=3 * sx * sy), :]
            edge[pl.ds(start + 2, cols, stride=SLAB), :] = high_ref[pl.ds(high_at + pick, cols, stride=3 * sx), :]
            edge[pl.ds(start + 3, cols, stride=SLAB), :] = high_ref[pl.ds(high_at + n + pick, cols, stride=3 * sx), :]

    def unpack_fields(layer, source, low, high, at):
        low_ref, low_at = low
        high_ref, high_at = high
        index = layer + 1
        stiff[pl.ds(index * sy, sy), :] = source[pl.ds(field + at * sy, sy), :]
        before = low_ref[pl.ds(low_at + n + at, 1), :]
        after = high_ref[pl.ds(high_at + 3 * n + at, 1), :]
        for j in range(4):
            row = before if j < 2 else after
            stiff_edge[pl.ds(index * SLAB + j, 3, stride=4), :] = jnp.broadcast_to(row, (3, sz))
        mass_rows[pl.ds(index * SLAB, 1), :] = low_ref[pl.ds(low_at + n + sx + at, 1), :]
        mass_rows[pl.ds(index * SLAB + 1, sy), :] = source[pl.ds(field + plane + at * sy, sy), :]
        mass_rows[pl.ds(index * SLAB + 1 + sy, 1), :] = high_ref[pl.ds(high_at + 3 * n + sx + at, 1), :]

    def unpack_nodes(layer, source, prev_source, high, at, prev_stride, prev_at):
        high_ref, high_at = high
        for k in range(cols):
            for d in range(3):
                basis[pl.ds(base(layer, 3 * cols + k, d), sy), :] = prev_source[
                    pl.ds(prev_at + ((k * 3 + d) * prev_stride) * sy, sy), :
                ]
        basis[pl.ds(base(layer, 3 * cols, 0) + sy, slabs, stride=span), :] = high_ref[
            pl.ds(high_at + 2 * n + at, slabs, stride=sx), :
        ]
        for d in range(3):
            scale[pl.ds((layer * 3 + d) * SLAB, sy), :] = source[pl.ds(field + 2 * plane + (d * sx + at) * sy, sy), :]
        scale[pl.ds(layer * 3 * SLAB + sy, 3, stride=SLAB), :] = high_ref[pl.ds(high_at + 3 * n + 2 * sx + at, 3, stride=sx), :]

    edge[...] = jnp.zeros(edge.shape, f32)
    stiff_edge[...] = jnp.zeros(stiff_edge.shape, f32)
    own_low = (from_low, 0)
    own_high = (from_high, 0)
    for layer in range(sx):
        unpack(layer, own, own_low, own_high, layer)
        unpack_fields(layer, own, own_low, own_high, layer)
        unpack_nodes(layer, own, prev_free, own_high, layer, sx, layer * sy)

    def unpack_sides(lower, lower_corner, upper, upper_corner):
        lower_high = (lower_corner, low_rows)
        unpack(-1, lower, (lower_corner, 0), lower_high, sx - 1)
        unpack_fields(-1, lower, (lower_corner, 0), lower_high, sx - 1)
        upper_high = (upper_corner, low_rows)
        for step in range(2):
            unpack(sx + step, upper, (upper_corner, 0), upper_high, step)
        unpack_fields(sx, upper, (upper_corner, 0), upper_high, 0)
        unpack_nodes(sx, upper, upper, upper_high, 0, 1, block)

    @pl.when(place[0] == 1)
    def _():
        unpack_sides(pair_a, corner_a, pair_b, corner_b)

    @pl.when(place[0] == 0)
    def _():
        unpack_sides(pair_b, corner_b, pair_a, corner_a)

    for layer in range(sx + 1):
        first = layer * SLAB
        second = first + SLAB
        mass_sum = mass_rows[pl.ds(first, SLAB), :] + mass_rows[pl.ds(second, SLAB), :]
        lumped[pl.ds(layer * SLAB, SLAB), :] = mass_sum
        inner = lumped[pl.ds(layer * SLAB, sy), :] + lumped[pl.ds(layer * SLAB + 1, sy), :]
        outer = lumped[pl.ds(layer * SLAB + sy, 1), :] + lumped[pl.ds(layer * SLAB + sy + 1, 1), :]
        lumped[pl.ds(layer * SLAB, sy), :] = inner + pltpu.roll(inner, 1, 1) * not_first
        outer = jnp.broadcast_to(outer, (8, sz))
        outer = outer + pltpu.roll(outer, 1, 1) * not_first
        lumped[pl.ds(layer * SLAB + sy, 1), :] = outer[0:1]

    def edge_tiles(k, layer):
        plain = stiff_edge[pl.ds((layer + 1) * SLAB, SLAB), :]
        cut = plain * jnp.concatenate([not_last, not_last], 0)
        tiles = []
        for a in range(2):
            tile = edge[pl.ds(((layer + 1 + a) * cols + k) * SLAB, SLAB), :]
            tiles.append(tile * plain)
            tiles.append(pltpu.roll(tile, sz - 1, 1) * cut)
        return tiles

    above[...] = jnp.zeros(above.shape, f32)
    below[...] = jnp.zeros(below.shape, f32)

    def current_pair(pair, carry):
        sums = [[0.0, 0.0], [0.0, 0.0]]
        tails = [None, None]
        for layer in range(-1, sx + 1):
            inner = 0 <= layer < sx
            columns = []
            kept = []
            for c in range(2):
                k = pair * 2 + c
                tiles = corner_tiles(k, layer)
                kept.append(tiles)
                columns.append(jnp.concatenate(scaled(tiles, layer) + edge_tiles(k, layer), 0))
            out, forces, doubled = apply(columns, NODE_ROWS + FORCE_ROWS if inner else NODE_ROWS, FORCE_ROWS + EDGE)
            for c in range(2):
                k = pair * 2 + c
                part = out[:, c * sz : (c + 1) * sz]
                if inner:
                    work = forces[:, c * sz : (c + 1) * sz] * doubled[:, c * sz : (c + 1) * sz]
                    energy = 0.0
                    square = [0.0, 0.0]
                    for alpha in range(24):
                        q = (alpha // 3) % 2
                        tile = kept[c][alpha]
                        energy = energy + work[alpha * sy : (alpha + 1) * sy]
                        square[q] = square[q] + tile * tile
                    at = (k * sx + layer) * sy
                    mass = mass_rows[pl.ds((layer + 1) * SLAB + 1, sy), :]
                    stiff_out[pl.ds(at, sy), :] = energy * (3.0 / weights(layer)[0])
                    mass_out[pl.ds(at, sy), :] = mass * (square[0] + square[1] * not_last)
                parts, rim = node_parts(part)
                if layer >= 0:
                    before, rim_before = tails[c]
                    rim_sum = rim[0:3] + rim_before[3:6]
                    load = lumped[pl.ds(layer * SLAB, SLAB), :]
                    for d in range(3):
                        total = parts[d] + before[3 + d]
                        factor = scale[pl.ds((layer * 3 + d) * SLAB, SLAB), :]
                        a_value = factor[0:sy] * total
                        both = factor * load
                        b_value = both[0:sy] * basis[pl.ds(base(layer, k, d), sy), :]
                        b_rim = both[sy : sy + 1] * basis[pl.ds(base(layer, k, d) + sy, 1), :]
                        basis[pl.ds(base(layer, cols + k, d), sy), :] = a_value
                        basis[pl.ds(base(layer, cols + k, d) + sy, 1), :] = factor[sy : sy + 1] * rim_sum[d : d + 1]
                        basis[pl.ds(base(layer, 2 * cols + k, d), sy), :] = b_value
                        basis[pl.ds(base(layer, 2 * cols + k, d) + sy, 1), :] = b_rim
                        if layer < sx:
                            value = basis[pl.ds(base(layer, k, d), sy), :]
                            sums[c][0] = sums[c][0] + value * total
                            sums[c][1] = sums[c][1] + value * value * load[0:sy]
                            applied[pl.ds(out_base(layer, k, d), sy), :] = total
                            at = ((k * 3 + d) * sx + layer) * sy
                            a_out[pl.ds(at, sy), :] = a_value
                            b_out[pl.ds(at, sy), :] = b_value
                        else:
                            applied[pl.ds(out_base(layer, k, d), sy), :] = jnp.zeros((sy, sz), f32)
                        applied[pl.ds(out_base(layer, k, d) + sy, 1), :] = jnp.zeros((1, sz), f32)
                tails[c] = (parts, rim)
        for c in range(2):
            above[pl.ds(pair * 2 + c, 1), :] = jnp.sum(sums[c][0], 0, keepdims=True)
            below[pl.ds(pair * 2 + c, 1), :] = jnp.sum(sums[c][1], 0, keepdims=True)
        return carry

    lax.fori_loop(0, cols // 2, current_pair, 0, unroll=cols // 2)

    half = sz // 2
    rows = cols * sx * sy
    wide = lax.broadcasted_iota(jnp.int32, (rows, sz), 1)
    stiff_all = stiff_out[...]
    mass_all = mass_out[...]
    first = place[1] == 0
    stiff_half = jnp.where(first, pltpu.roll(stiff_all, half, 1), stiff_all)
    mass_half = jnp.where(first, mass_all, pltpu.roll(mass_all, half, 1))
    share_out[0:rows] = jnp.where(wide < half, stiff_half, mass_half)
    spot = lax.broadcasted_iota(jnp.int32, above.shape, 1)
    top = jnp.sum(above[...], 1, keepdims=True)
    bottom = jnp.sum(below[...], 1, keepdims=True)
    share_out[rows:] = jnp.where(spot == OTHER_TOP, top, 0.0) + jnp.where(spot == OTHER_TOP + 1, bottom, 0.0)


def gram_kernel(sizes, basis, stiff, lumped, op_high, op_low, applied_in, applied, gram_out):
    cols, sx, sy, sz = sizes
    width = 4 * cols
    span = sy + 1
    base, out_base, _, _, corner_tiles, _, scaled, apply, node_parts = helpers(sizes, basis, stiff, op_high, op_low)

    def other_pair(pair, carry):
        tails = [None, None]
        for layer in range(sx):
            columns = []
            for c in range(2):
                k = cols + pair * 2 + c
                columns.append(jnp.concatenate(scaled(corner_tiles(k, layer), layer), 0))
            out = apply(columns, NODE_ROWS, FORCE_ROWS)[0]
            for c in range(2):
                k = cols + pair * 2 + c
                parts, rim = node_parts(out[:, c * sz : (c + 1) * sz])
                ends = [(layer, parts[0:3], rim[0:3], tails[c])]
                if layer == sx - 1:
                    ends.append((sx, parts[3:6], rim[3:6], None))
                for at, values, row, before in ends:
                    for d in range(3):
                        value = values[d]
                        last = row[d : d + 1]
                        if before is not None:
                            value = value + before[0][3 + d]
                            last = last + before[1][3 + d : 4 + d]
                        applied[pl.ds(out_base(at, k, d), sy), :] = value
                        applied[pl.ds(out_base(at, k, d) + sy, 1), :] = last
                tails[c] = (parts, rim)
        return carry

    lax.fori_loop(0, 3 * cols // 2, other_pair, 0, unroll=3 * cols // 2)

    def contract(left, right):
        return lax.dot_general(left, right, (((1,), (1,)), ((), ())), preferred_element_type=f32)

    step = 3 * span

    def product(applied_values, basis_values):
        left_high, left_low = split(jnp.concatenate(basis_values, 1))
        right_high, right_low = split(jnp.concatenate(applied_values, 1))
        rows = left_high.shape[0]
        both = contract(jnp.concatenate([left_high, left_low], 0), right_high)
        return both[0:rows] + both[rows:] + contract(left_high, right_low)

    def gram_group(index, carry):
        layer = index // 3
        d = index - layer * 3
        values = []
        others = []
        for y in range(sy):
            value = basis[pl.ds(((layer + 1) * width * 3 + d) * span + y, width, stride=step), :]
            other = applied[pl.ds((layer * width * 3 + d) * span + y, width, stride=step), :]
            values.append(value)
            others.append(jnp.concatenate([other, value * lumped[pl.ds(layer * SLAB + y, 1), :]], 0))
        return carry + product(others, values)

    both = lax.fori_loop(0, 3 * sx, gram_group, jnp.zeros((width, 2 * width), f32))

    def gram_end(d, carry):
        values = []
        others = []
        for y in range(sy):
            values.append(basis[pl.ds(((sx + 1) * width * 3 + d) * span + y, width, stride=step), :])
            others.append(applied[pl.ds((sx * width * 3 + d) * span + y, width, stride=step), :])
        return carry + product(others, values)

    gram_stiff = lax.fori_loop(0, 3, gram_end, both[:, 0:width])
    values = []
    others = []
    for layer in range(sx + 1):
        for d in range(3):
            values.append(basis[pl.ds(base(layer, 0, d) + sy, width, stride=step), :])
            others.append(applied[pl.ds(out_base(layer, 0, d) + sy, width, stride=step), :])
    gram_stiff = gram_stiff + product(others, values)
    gram_out[...] = jnp.zeros(gram_out.shape, f32)
    gram_out[:, 0:width] = gram_stiff
    gram_out[:, 64 : 64 + width] = both[:, width : 2 * width]


def finish_kernel(
    sizes, dof, place, gram, a_in, b_in, stiff_in, mass_in, other, stiff_gram, mass_gram, search, sensitivity
):
    cols, sx, sy, sz = sizes
    eye = (
        lax.broadcasted_iota(jnp.int32, (cols, cols), 0) == lax.broadcasted_iota(jnp.int32, (cols, cols), 1)
    ).astype(f32)
    top = gram[0:cols, 0:cols] * eye
    bottom = gram[0:cols, 64 : 64 + cols] * eye
    quotient = jnp.sum(top, 1, keepdims=True) / jnp.sum(bottom, 1, keepdims=True)
    quotient_row = jnp.sum(top, 0, keepdims=True) / jnp.sum(bottom, 0, keepdims=True)
    for at, out in ((0, stiff_gram), (64, mass_gram)):
        whole = gram[:, at : at + 4 * cols]
        rows = jnp.concatenate(
            [whole[0:cols], whole[cols : 2 * cols] - quotient * whole[2 * cols : 3 * cols], whole[3 * cols :]], 0
        )
        out[:, 0, :] = (1.0 / dof) * jnp.concatenate(
            [
                rows[:, 0:cols],
                rows[:, cols : 2 * cols] - quotient_row * rows[:, 2 * cols : 3 * cols],
                rows[:, 3 * cols :],
            ],
            1,
        )

    def weigh(value, total):
        squared = value * value
        powered = 1.0 / (squared * squared)
        factor = powered / (total * (1.0 / dof))
        return jnp.sum(powered, 0, keepdims=True), factor, factor * value

    overall, coefficient, weighted = weigh(quotient, jnp.sum(bottom, 1, keepdims=True))
    other_total = gram[0:cols, OTHER_TOP + 1 : OTHER_TOP + 2]
    other_sum, other_coefficient, other_weighted = weigh(gram[0:cols, OTHER_TOP : OTHER_TOP + 1] / other_total, other_total)
    half = sz // 2
    spot = lax.broadcasted_iota(jnp.int32, (cols, sz), 1)
    other_factor = jnp.where(spot < half, other_coefficient, -other_weighted)
    plane = sx * sy
    mine = 0.0
    received = 0.0
    for j in range(cols):
        here = pl.ds(j * 3 * plane, 3 * plane)
        value = a_in[here, :] - quotient[j : j + 1] * b_in[here, :]
        search[0, j] = value.reshape(3, sx, sy, sz)
        part = pl.ds(j * plane, plane)
        mine = mine + coefficient[j : j + 1] * stiff_in[part, :] - weighted[j : j + 1] * mass_in[part, :]
        received = received + other_factor[j : j + 1] * other[part, :]
    received = received + pltpu.roll(received, half, 1)
    mine = jnp.where(place[1] == 0, mine, pltpu.roll(mine, half, 1))
    total = (mine + received) / (overall + other_sum)
    sensitivity[...] = total[:, 0:half].reshape(sx, sy, half)


def line(axis, step):
    count = lax.axis_size(axis)
    return [(i, i + step) for i in range(count) if 0 <= i + step < count]


def pairs(axis, first):
    count = lax.axis_size(axis)
    steps = []
    for i in range(first, count - 1, 2):
        steps += [(i, i + 1), (i + 1, i)]
    return steps


def sum_over(value, axis):
    count = lax.axis_size(axis)
    if count & (count - 1):
        return lax.psum(value, axis)
    distance = 1
    while distance < count:
        value = value + lax.ppermute(value, axis, [(i, i ^ distance) for i in range(count)])
        distance *= 2
    return value


def near(value):
    return pltpu.with_memory_space_constraint(value, pltpu.VMEM)


def far(value):
    return pltpu.with_memory_space_constraint(value, pltpu.HBM)


def shards(current, previous, element_stiffness, preconditioner, modulus, density, solid, clamped):
    cols = current.shape[1]
    sx, sy, sz = modulus.shape
    sizes = (cols, sx, sy, sz)
    slabs = cols * 3
    n = slabs * sx
    block = n * sy
    dof = 3.0 * sx * sy * sz * lax.axis_size("bx") * lax.axis_size("by")

    def struct(*shape):
        return jax.ShapeDtypeStruct(shape, f32)

    def kept(*shape, dtype=f32):
        return pltpu.VMEM(shape, dtype)

    own_rows = block + slabs * sy + 5 * sx * sy
    up_rows = -(-(n + 2 * sx) // 8) * 8
    down_rows = -(-(3 * n + 5 * sx) // 8) * 8
    sources = (current, previous, modulus, density, solid, preconditioner, clamped)
    own, prev_free, up, down = pl.pallas_call(
        lambda *refs: prepare_kernel(sizes, *refs),
        in_specs=[pl.BlockSpec(memory_space=pltpu.HBM)] * len(sources),
        scratch_shapes=[pltpu.VMEM(x.shape, x.dtype) for x in sources] + [pltpu.SemaphoreType.DMA((len(sources),))],
        out_shape=(kept(own_rows, sz), kept(block, sz), kept(up_rows, sz), kept(down_rows, sz)),
        compiler_params=pltpu.CompilerParams(vmem_limit_bytes=12 << 20),
        name="prepare",
    )(*[far(x) for x in sources])
    from_low = lax.ppermute(up, "by", line("by", 1))
    from_high = lax.ppermute(down, "by", line("by", -1))
    row_pick, col_pick, op_mask = operator_tables(sy)
    tables = (element_stiffness, jnp.asarray(row_pick, bf16), jnp.asarray(col_pick, bf16), jnp.asarray(op_mask, bf16))
    op_high, op_low = pl.pallas_call(
        operator_kernel,
        in_specs=[pl.BlockSpec(memory_space=pltpu.HBM)] * len(tables),
        out_shape=(kept(NODE_ROWS + FORCE_ROWS, FORCE_ROWS + EDGE, dtype=bf16),) * 2,
        scratch_shapes=[pltpu.VMEM(x.shape, x.dtype) for x in tables] + [pltpu.SemaphoreType.DMA((len(tables),))],
        compiler_params=pltpu.CompilerParams(vmem_limit_bytes=8 << 20),
        name="operator",
    )(*[far(x) for x in tables])
    pair_a = lax.ppermute(own, "bx", pairs("bx", 0))
    pair_b = lax.ppermute(own, "bx", pairs("bx", 1))
    from_low, from_high, op_high, op_low = lax.optimization_barrier((from_low, from_high, op_high, op_low))
    corner = jnp.concatenate([from_low, from_high], 0)
    corner_a = lax.ppermute(corner, "bx", pairs("bx", 0))
    corner_b = lax.ppermute(corner, "bx", pairs("bx", 1))
    place = jnp.stack([lax.axis_index("bx") % 2, lax.axis_index("real")]).astype(jnp.int32)
    width = 4 * cols
    span = sy + 1
    energies = cols * sx * sy
    vmem = pl.BlockSpec(memory_space=pltpu.VMEM)
    smem = pl.BlockSpec(memory_space=pltpu.SMEM)
    basis, applied, a_part, b_part, stiff_part, mass_part, shared, stiff, lumped = pl.pallas_call(
        lambda *refs: current_kernel(sizes, *refs),
        in_specs=[smem] + [vmem] * 10,
        out_shape=(
            kept((sx + 3) * width * 3 * span, sz),
            kept((sx + 1) * width * 3 * span, sz),
            kept(block, sz),
            kept(block, sz),
            kept(energies, sz),
            kept(energies, sz),
            kept(energies + 16, sz),
            kept((sx + 2) * sy, sz),
            kept((sx + 1) * SLAB, sz),
        ),
        scratch_shapes=[
            pltpu.VMEM(((sx + 3) * cols * SLAB, sz), f32),
            pltpu.VMEM(((sx + 2) * SLAB, sz), f32),
            pltpu.VMEM(((sx + 2) * SLAB, sz), f32),
            pltpu.VMEM(((sx + 1) * 3 * SLAB, sz), f32),
            pltpu.VMEM((16, sz), f32),
            pltpu.VMEM((16, sz), f32),
        ],
        compiler_params=pltpu.CompilerParams(vmem_limit_bytes=16 << 20),
        name="current",
    )(place, *[near(x) for x in (own, prev_free, from_low, from_high, pair_a, pair_b, corner_a, corner_b, op_high, op_low)])
    count = lax.axis_size("real")
    other = lax.ppermute(shared, "real", [(i, (i + 1) % count) for i in range(count)])
    _, gram = pl.pallas_call(
        lambda *refs: gram_kernel(sizes, *refs),
        in_specs=[vmem] * 6,
        out_shape=(kept((sx + 1) * width * 3 * span, sz), kept(width, 128)),
        input_output_aliases={5: 0},
        compiler_params=pltpu.CompilerParams(vmem_limit_bytes=16 << 20),
        name="gram",
    )(*[near(x) for x in (basis, stiff, lumped, op_high, op_low, applied)])
    gram = jnp.concatenate([gram[0:16] + other[energies:], gram[16:]], 0)
    gram = sum_over(sum_over(gram, "bx"), "by")
    stiff_gram, mass_gram, search, sensitivity = pl.pallas_call(
        lambda *refs: finish_kernel(sizes, dof, *refs),
        in_specs=[smem] + [vmem] * 6,
        out_shape=(
            struct(3 * cols, 1, 3 * cols),
            struct(3 * cols, 1, 3 * cols),
            struct(1, cols, 3, sx, sy, sz),
            struct(sx, sy, sz // 2),
        ),
        compiler_params=pltpu.CompilerParams(vmem_limit_bytes=12 << 20),
        name="finish",
    )(place, *[near(x) for x in (gram, a_part, b_part, stiff_part, mass_part, other)])
    return jnp.swapaxes(stiff_gram, 0, 1), jnp.swapaxes(mass_gram, 0, 1), search, sensitivity


def solution(mesh):
    in_specs = (
        P("real", None, None, "bx", "by", None),
        P("real", None, None, "bx", "by", None),
        P(),
        P("real", None, "bx", "by", None),
        P("bx", "by", None),
        P("bx", "by", None),
        P("real", "bx", "by", None),
        P("bx", "by"),
    )
    out_specs = (
        P("real", None, None),
        P("real", None, None),
        P("real", None, None, "bx", "by", None),
        P("bx", "by", "real"),
    )
    return jax.shard_map(shards, mesh=mesh, in_specs=in_specs, out_specs=out_specs, check_vma=False)
```

profile of v0, /device:TPU:0, one launch (start us, length us, event | category | flops | bytes accessed | tf_op | source)
XLA Modules:
  0.0 45.6 jit_solution(11492176809614345968)
XLA Ops:
  0.6 1.3 %prepare.1 = (f32[944,128]{1,0:T(8,128)S(1)}, f32[576,128]{1,0:T(8,128)S(1)}, f32[80,128]{1,0:T(8,128)S(1)}, f32[232,128]{1,0:T(8,128)S(1)}) custom-call(f32[1,12,3,2,8,128]{5,4,3,2,1,0:T(8,128)} %refs_0_.2, f32[1,12,3,2,8,128]{5,4,3,2,1,0:T(8,128)} %refs_1_.2, f32[2,8,128]{2,1,0:T(8,128)} %refs_2_.2, f32[2,8,128]{2,1,0:T(8,128)} %refs_3_.2, ...), custom_call_target="tpu_custom_call" | custom-call | tf_op jit(solution)/shard_map/prepare/pallas_call | solution.py:546
  1.9 1.3 %collective-permute-start.1 = (f32[232,128]{1,0:T(8,128)S(1)}, f32[232,128]{1,0:T(8,128)S(1)}, u32[]{:S(2)}, u32[]{:S(2)}) collective-permute-start(f32[232,128]{1,0:T(8,128)S(1)} %get-tuple-element.31), channel_id=1, source_target_pairs={{1,0},{2,1},{3,2},{5,4},{6,5},{7,6},{9,8},{10,9},{11,10},{13,12},{... | collective-permute-start | bytes 356360 | tf_op jit(solution)/shard_map/ppermute | solution.py:555
  3.2 0.7 %collective-permute-start.3 = (f32[944,128]{1,0:T(8,128)S(1)}, f32[944,128]{1,0:T(8,128)S(1)}, u32[]{:S(2)}, u32[]{:S(2)}) collective-permute-start(f32[944,128]{1,0:T(8,128)S(1)} %get-tuple-element.28.refs_1_), channel_id=1, source_target_pairs={{4,8},{8,4},{5,9},{9,5},{6,10},{10,6},{7,11},{11,7},{20,24},{24,20... | collective-permute-start | bytes 1449992 | tf_op jit(solution)/shard_map/ppermute | solution.py:567
  3.9 4.4 %collective-permute-start.2 = (f32[944,128]{1,0:T(8,128)S(1)}, f32[944,128]{1,0:T(8,128)S(1)}, u32[]{:S(2)}, u32[]{:S(2)}) collective-permute-start(f32[944,128]{1,0:T(8,128)S(1)} %get-tuple-element.28.refs_1_), channel_id=1, source_target_pairs={{0,4},{4,0},{8,12},{12,8},{1,5},{5,1},{9,13},{13,9},{2,6},{6,2},{1... | collective-permute-start | bytes 1449992 | tf_op jit(solution)/shard_map/ppermute | solution.py:566
  8.3 4.5 %collective-permute-start = (f32[80,128]{1,0:T(8,128)S(1)}, f32[80,128]{1,0:T(8,128)S(1)}, u32[]{:S(2)}, u32[]{:S(2)}) collective-permute-start(f32[80,128]{1,0:T(8,128)S(1)} %get-tuple-element.30), channel_id=1, source_target_pairs={{0,1},{1,2},{2,3},{4,5},{5,6},{6,7},{8,9},{9,10},{10,11},{12,13},{... | collective-permute-start | bytes 122888 | tf_op jit(solution)/shard_map/ppermute | solution.py:554
  12.8 1.7 %operator.1 = (bf16[304,256]{1,0:T(8,128)(2,1)S(1)}, bf16[304,256]{1,0:T(8,128)(2,1)S(1)}) custom-call(f32[24,24]{1,0:T(8,128)} %refs_0_.3, bf16[2,304,24]{2,1,0:T(8,128)(2,1)} %constant.30.clone.refs_1_, bf16[24,256]{1,0:T(8,128)(2,1)} %constant.31.clone.refs_2_, bf16[2,304,256]{2,1,0:T(8,128)(2,1)} %constant.32.clone.refs_3_), custom_call_target="tpu_custom_call" | custom-call | tf_op jit(solution)/shard_map/operator/pallas_call | solution.py:558
  14.5 0.0 collective-permute-done.refs_3_
  14.6 0.7 %collective-permute-start.5 = (f32[312,128]{1,0:T(8,128)S(1)}, f32[312,128]{1,0:T(8,128)S(1)}, u32[]{:S(2)}, u32[]{:S(2)}) collective-permute-start(f32[312,128]{1,0:T(8,128)S(1)} %constant_dynamic-update-slice_fusion), channel_id=1, source_target_pairs={{4,8},{8,4},{5,9},{9,5},{6,10},{10,6},{7,11},{11,7},{20,24},{24,20... | collective-permute-start | bytes 479240 | tf_op jit(solution)/shard_map/ppermute | solution.py:571
  15.3 1.3 %collective-permute-start.4 = (f32[312,128]{1,0:T(8,128)S(1)}, f32[312,128]{1,0:T(8,128)S(1)}, u32[]{:S(2)}, u32[]{:S(2)}) collective-permute-start(f32[312,128]{1,0:T(8,128)S(1)} %constant_dynamic-update-slice_fusion), channel_id=1, source_target_pairs={{0,4},{4,0},{8,12},{12,8},{1,5},{5,1},{9,13},{13,9},{2,6},{6,2},{1... | collective-permute-start | bytes 479240 | tf_op jit(solution)/shard_map/ppermute | solution.py:570
  16.6 0.1 pad_add_fusion.refs_0_
  16.7 0.9 %collective-permute-done.4.refs_7_ = f32[312,128]{1,0:T(8,128)S(1)} collective-permute-done((f32[312,128]{1,0:T(8,128)S(1)}, f32[312,128]{1,0:T(8,128)S(1)}, u32[]{:S(2)}, u32[]{:S(2)}) %collective-permute-start.4) | collective-permute-done | bytes 159776 | tf_op jit(solution)/shard_map/ppermute | solution.py:570
  17.6 3.5 %current.1 = (f32[6480,128]{1,0:T(8,128)S(1)}, f32[3888,128]{1,0:T(8,128)S(1)}, f32[576,128]{1,0:T(8,128)S(1)}, f32[576,128]{1,0:T(8,128)S(1)}, f32[192,128]{1,0...) custom-call(s32[2]{0:T(128)S(1)} %pad_add_fusion.refs_0_, ...), custom_call_target="tpu_custom_call" | custom-call | tf_op jit(solution)/shard_map/current/pallas_call | solution.py:578
  21.1 1.5 %collective-permute-start.6 = (f32[208,128]{1,0:T(8,128)S(1)}, f32[208,128]{1,0:T(8,128)S(1)}, u32[]{:S(2)}, u32[]{:S(2)}) collective-permute-start(f32[208,128]{1,0:T(8,128)S(1)} %get-tuple-element.43), channel_id=1, source_target_pairs={{0,16},{16,0},{1,17},{17,1},{2,18},{18,2},{3,19},{19,3},{4,20},{20... | collective-permute-start | bytes 319496 | tf_op jit(solution)/shard_map/ppermute | solution.py:604
  22.6 4.8 %gram.1 = (f32[3888,128]{1,0:T(8,128)S(1)}, f32[48,128]{1,0:T(8,128)S(1)}) custom-call(f32[6480,128]{1,0:T(8,128)S(1)} %get-tuple-element.38.refs_0_, f32[32,128]{1,0:T(8,128)S(1)} %get-tuple-element.39.refs_1_, f32[48,128]{1,0:T(8,128)S(1)} %get-tuple-element.40.refs_2_, ...), custom_call_target="tpu_custom_call", output_to_operand_aliasing={{0}: (5, {})} | custom-call | tf_op jit(solution)/shard_map/gram/pallas_call | solution.py:605
  27.5 0.0 collective-permute-done.6.refs_6_
  27.5 3.1 %collective-permute-start.7 = (f32[48,128]{1,0:T(8,128)S(1)}, f32[48,128]{1,0:T(8,128)S(1)}, u32[]{:S(2)}, u32[]{:S(2)}) collective-permute-start(f32[48,128]{1,0:T(8,128)S(1)} %pad_maximum_fusion), channel_id=1, source_target_pairs={{0,4},{4,0},{8,12},{12,8},{1,5},{5,1},{9,13},{13,9},{2,6},{6,2},{1... | collective-permute-start | bytes 73736 | tf_op jit(solution)/shard_map/ppermute | solution.py:514
  30.6 0.8 %collective-permute-done.7 = f32[48,128]{1,0:T(8,128)S(1)} collective-permute-done((f32[48,128]{1,0:T(8,128)S(1)}, f32[48,128]{1,0:T(8,128)S(1)}, u32[]{:S(2)}, u32[]{:S(2)}) %collective-permute-start.7) | collective-permute-done | bytes 24608 | tf_op jit(solution)/shard_map/ppermute | solution.py:514
  31.5 0.8 %collective-permute-start.8 = (f32[48,128]{1,0:T(8,128)S(1)}, f32[48,128]{1,0:T(8,128)S(1)}, u32[]{:S(2)}, u32[]{:S(2)}) collective-permute-start(f32[48,128]{1,0:T(8,128)S(1)} %fusion), channel_id=1, source_target_pairs={{0,8},{4,12},{8,0},{12,4},{1,9},{5,13},{9,1},{13,5},{2,10},{6,14},... | collective-permute-start | bytes 73736 | tf_op jit(solution)/shard_map/ppermute | solution.py:514
  32.3 3.0 %collective-permute-done.8 = f32[48,128]{1,0:T(8,128)S(1)} collective-permute-done((f32[48,128]{1,0:T(8,128)S(1)}, f32[48,128]{1,0:T(8,128)S(1)}, u32[]{:S(2)}, u32[]{:S(2)}) %collective-permute-start.8) | collective-permute-done | bytes 24608 | tf_op jit(solution)/shard_map/ppermute | solution.py:514
  35.3 1.6 %collective-permute-start.9 = (f32[48,128]{1,0:T(8,128)S(1)}, f32[48,128]{1,0:T(8,128)S(1)}, u32[]{:S(2)}, u32[]{:S(2)}) collective-permute-start(f32[48,128]{1,0:T(8,128)S(1)} %add.22), channel_id=1, source_target_pairs={{0,1},{1,0},{2,3},{3,2},{4,5},{5,4},{6,7},{7,6},{8,9},{9,8},{10,11... | collective-permute-start | bytes 73736 | tf_op jit(solution)/shard_map/ppermute | solution.py:514
  36.9 2.2 %collective-permute-done.9 = f32[48,128]{1,0:T(8,128)S(1)} collective-permute-done((f32[48,128]{1,0:T(8,128)S(1)}, f32[48,128]{1,0:T(8,128)S(1)}, u32[]{:S(2)}, u32[]{:S(2)}) %collective-permute-start.9) | collective-permute-done | bytes 24608 | tf_op jit(solution)/shard_map/ppermute | solution.py:514
  39.1 2.6 %collective-permute-start.10 = (f32[48,128]{1,0:T(8,128)S(1)}, f32[48,128]{1,0:T(8,128)S(1)}, u32[]{:S(2)}, u32[]{:S(2)}) collective-permute-start(f32[48,128]{1,0:T(8,128)S(1)} %add.23), channel_id=1, source_target_pairs={{0,2},{1,3},{2,0},{3,1},{4,6},{5,7},{6,4},{7,5},{8,10},{9,11},{10,... | collective-permute-start | bytes 73736 | tf_op jit(solution)/shard_map/ppermute | solution.py:514
  41.7 2.1 %collective-permute-done.10 = f32[48,128]{1,0:T(8,128)S(1)} collective-permute-done((f32[48,128]{1,0:T(8,128)S(1)}, f32[48,128]{1,0:T(8,128)S(1)}, u32[]{:S(2)}, u32[]{:S(2)}) %collective-permute-start.10) | collective-permute-done | bytes 24608 | tf_op jit(solution)/shard_map/ppermute | solution.py:514
  43.9 1.8 %finish.1 = (f32[36,1,36]{2,1,0:T(1,128)}, f32[36,1,36]{2,1,0:T(1,128)}, f32[1,12,3,2,8,128]{5,4,3,2,1,0:T(8,128)}, f32[2,8,64]{2,1,0:T(8,128)}) custom-call(s32[2]{0:T(128)S(1)} %pad_add_fusion.refs_0_, f32[48,128]{1,0:T(8,128)S(1)} %add.24.refs_1_, f32[576,128]{1,0:T(8,128)S(1)} %get-tuple-element.44.refs_2_, f32[576,128]{1,0:T(8,128)S(1)} %get-tuple-element.45.refs_3_, ...), custom_call_target="tpu_custom_call" | custom-call | tf_op jit(solution)/shard_map/finish/pallas_call | solution.py:615
  (13 shorter events, 0.1 us)
Async XLA Ops:
  1.9 12.6 %collective-permute-start.1 = (f32[232,128]{1,0:T(8,128)S(1)}, f32[232,128]{1,0:T(8,128)S(1)}, u32[]{:S(2)}, u32[]{:S(2)}) collective-permute-start(f32[232,128]{1,0:T(8,128)S(1)} %get-tuple-element.31), channel_id=1, source_target_pairs={{1,0},{2,1},{3,2},{5,4},{6,5},{7,6},{9,8},{10,9},{11,10},{13,12},{... | collective-permute-start | bytes 356360 | tf_op jit(solution)/shard_map/ppermute | solution.py:555
  3.2 14.4 %collective-permute-start.3 = (f32[944,128]{1,0:T(8,128)S(1)}, f32[944,128]{1,0:T(8,128)S(1)}, u32[]{:S(2)}, u32[]{:S(2)}) collective-permute-start(f32[944,128]{1,0:T(8,128)S(1)} %get-tuple-element.28.refs_1_), channel_id=1, source_target_pairs={{4,8},{8,4},{5,9},{9,5},{6,10},{10,6},{7,11},{11,7},{20,24},{24,20... | collective-permute-start | bytes 1449992 | tf_op jit(solution)/shard_map/ppermute | solution.py:567
  3.9 13.7 %collective-permute-start.2 = (f32[944,128]{1,0:T(8,128)S(1)}, f32[944,128]{1,0:T(8,128)S(1)}, u32[]{:S(2)}, u32[]{:S(2)}) collective-permute-start(f32[944,128]{1,0:T(8,128)S(1)} %get-tuple-element.28.refs_1_), channel_id=1, source_target_pairs={{0,4},{4,0},{8,12},{12,8},{1,5},{5,1},{9,13},{13,9},{2,6},{6,2},{1... | collective-permute-start | bytes 1449992 | tf_op jit(solution)/shard_map/ppermute | solution.py:566
  8.3 6.2 %collective-permute-start = (f32[80,128]{1,0:T(8,128)S(1)}, f32[80,128]{1,0:T(8,128)S(1)}, u32[]{:S(2)}, u32[]{:S(2)}) collective-permute-start(f32[80,128]{1,0:T(8,128)S(1)} %get-tuple-element.30), channel_id=1, source_target_pairs={{0,1},{1,2},{2,3},{4,5},{5,6},{6,7},{8,9},{9,10},{10,11},{12,13},{... | collective-permute-start | bytes 122888 | tf_op jit(solution)/shard_map/ppermute | solution.py:554
  14.6 2.1 %collective-permute-start.5 = (f32[312,128]{1,0:T(8,128)S(1)}, f32[312,128]{1,0:T(8,128)S(1)}, u32[]{:S(2)}, u32[]{:S(2)}) collective-permute-start(f32[312,128]{1,0:T(8,128)S(1)} %constant_dynamic-update-slice_fusion), channel_id=1, source_target_pairs={{4,8},{8,4},{5,9},{9,5},{6,10},{10,6},{7,11},{11,7},{20,24},{24,20... | collective-permute-start | bytes 479240 | tf_op jit(solution)/shard_map/ppermute | solution.py:571
  15.3 2.4 %collective-permute-start.4 = (f32[312,128]{1,0:T(8,128)S(1)}, f32[312,128]{1,0:T(8,128)S(1)}, u32[]{:S(2)}, u32[]{:S(2)}) collective-permute-start(f32[312,128]{1,0:T(8,128)S(1)} %constant_dynamic-update-slice_fusion), channel_id=1, source_target_pairs={{0,4},{4,0},{8,12},{12,8},{1,5},{5,1},{9,13},{13,9},{2,6},{6,2},{1... | collective-permute-start | bytes 479240 | tf_op jit(solution)/shard_map/ppermute | solution.py:570
  21.1 6.4 %collective-permute-start.6 = (f32[208,128]{1,0:T(8,128)S(1)}, f32[208,128]{1,0:T(8,128)S(1)}, u32[]{:S(2)}, u32[]{:S(2)}) collective-permute-start(f32[208,128]{1,0:T(8,128)S(1)} %get-tuple-element.43), channel_id=1, source_target_pairs={{0,16},{16,0},{1,17},{17,1},{2,18},{18,2},{3,19},{19,3},{4,20},{20... | collective-permute-start | bytes 319496 | tf_op jit(solution)/shard_map/ppermute | solution.py:604
  27.5 3.9 %collective-permute-start.7 = (f32[48,128]{1,0:T(8,128)S(1)}, f32[48,128]{1,0:T(8,128)S(1)}, u32[]{:S(2)}, u32[]{:S(2)}) collective-permute-start(f32[48,128]{1,0:T(8,128)S(1)} %pad_maximum_fusion), channel_id=1, source_target_pairs={{0,4},{4,0},{8,12},{12,8},{1,5},{5,1},{9,13},{13,9},{2,6},{6,2},{1... | collective-permute-start | bytes 73736 | tf_op jit(solution)/shard_map/ppermute | solution.py:514
  31.5 3.8 %collective-permute-start.8 = (f32[48,128]{1,0:T(8,128)S(1)}, f32[48,128]{1,0:T(8,128)S(1)}, u32[]{:S(2)}, u32[]{:S(2)}) collective-permute-start(f32[48,128]{1,0:T(8,128)S(1)} %fusion), channel_id=1, source_target_pairs={{0,8},{4,12},{8,0},{12,4},{1,9},{5,13},{9,1},{13,5},{2,10},{6,14},... | collective-permute-start | bytes 73736 | tf_op jit(solution)/shard_map/ppermute | solution.py:514
  35.3 3.8 %collective-permute-start.9 = (f32[48,128]{1,0:T(8,128)S(1)}, f32[48,128]{1,0:T(8,128)S(1)}, u32[]{:S(2)}, u32[]{:S(2)}) collective-permute-start(f32[48,128]{1,0:T(8,128)S(1)} %add.22), channel_id=1, source_target_pairs={{0,1},{1,0},{2,3},{3,2},{4,5},{5,4},{6,7},{7,6},{8,9},{9,8},{10,11... | collective-permute-start | bytes 73736 | tf_op jit(solution)/shard_map/ppermute | solution.py:514
  39.1 4.7 %collective-permute-start.10 = (f32[48,128]{1,0:T(8,128)S(1)}, f32[48,128]{1,0:T(8,128)S(1)}, u32[]{:S(2)}, u32[]{:S(2)}) collective-permute-start(f32[48,128]{1,0:T(8,128)S(1)} %add.23), channel_id=1, source_target_pairs={{0,2},{1,3},{2,0},{3,1},{4,6},{5,7},{6,4},{7,5},{8,10},{9,11},{10,... | collective-permute-start | bytes 73736 | tf_op jit(solution)/shard_map/ppermute | solution.py:514
where the time goes:
time: 45.9 us; the launch traced here: 45.6 us
  starting transfers between devices  22.5 us (49%)
  Pallas kernels  13 us (28%)
  waiting for transfers between devices  9.2 us (20%)
  between operations  0.76 us (2%)
    ppermute x4, waiting for transfers between devices, sum_over(): lax.ppermute(value, axis, [(i, i ^ distance) for i in range(count)])  8.24 us
    ppermute x4, starting transfers between devices, sum_over(): lax.ppermute(value, axis, [(i, i ^ distance) for i in range(count)])  8.09 us
    pallas_call x1, Pallas kernels, shards(): pl.pallas_call(lambda *refs: gram_kernel(sizes, *refs), in_specs=[vmem] *...  4.84 us
    ppermute x1, starting transfers between devices, shards(): from_low = lax.ppermute(up, 'by', line('by', 1))  4.54 us
    ppermute x1, starting transfers between devices, shards(): pair_a = lax.ppermute(own, 'bx', pairs('bx', 0))  4.39 us
    pallas_call x1, Pallas kernels, shards(): pl.pallas_call(lambda *refs: current_kernel(sizes, *refs), in_specs=[smem...  3.46 us
    pallas_call x1, Pallas kernels, shards(): pl.pallas_call(lambda *refs: finish_kernel(sizes, dof, *refs), in_specs=[...  1.77 us
    pallas_call x1, Pallas kernels, shards(): pl.pallas_call(operator_kernel, in_specs=[pl.BlockSpec(memory_space=pltpu...  1.68 us
  transfers between devices with their start and end apart: 11, of which 5 were waited for; matrix products, arithmetic and copies ran while one was open for 0% of the time, Pallas kernels for 14%

commit v1 on v0

--- a/solution.py
+++ b/solution.py
@@ -79,8 +79,8 @@
         out[...] = total.astype(bf16)
 
 
-def prepare_kernel(sizes, *refs):
-    own, prev_free, up, down = refs[7:11]
+def prepare_kernel(sizes, odd, *refs):
+    own, prev_free, message_a, message_b = refs[7:11]
     cur, prev, modulus, density, solid, precond, clamped = fetch(refs[0:7], refs[11:18], refs[18])
     cols, sx, sy, sz = sizes
     slabs = cols * 3
@@ -104,14 +104,22 @@
     own[field + plane : field + 2 * plane] = (density[...] * (0.1 + 0.9 * share) * 0.125).reshape(plane, sz)
     own[field + 2 * plane : field + 5 * plane] = (precond[0] * free[None]).reshape(3 * plane, sz)
     n = slabs * sx
-    up[0:n] = own[pl.ds(sy - 1, n, stride=sy), :]
-    up[n : n + 2 * sx] = own[pl.ds(field + sy - 1, 2 * sx, stride=sy), :]
-    up[n + 2 * sx :] = jnp.zeros((up.shape[0] - n - 2 * sx, sz), f32)
-    down[0:n] = own[pl.ds(0, n, stride=sy), :]
-    down[n : 2 * n] = own[pl.ds(1, n, stride=sy), :]
-    down[2 * n : 3 * n] = prev_free[pl.ds(0, n, stride=sy), :]
-    down[3 * n : 3 * n + 5 * sx] = own[pl.ds(field, 5 * sx, stride=sy), :]
-    down[3 * n + 5 * sx :] = jnp.zeros((down.shape[0] - 3 * n - 5 * sx, sz), f32)
+
+    def fill(up, down):
+        up[0:n] = own[pl.ds(sy - 1, n, stride=sy), :]
+        up[n : n + 2 * sx] = own[pl.ds(field + sy - 1, 2 * sx, stride=sy), :]
+        down[0:n] = own[pl.ds(0, n, stride=sy), :]
+        down[n : 2 * n] = own[pl.ds(1, n, stride=sy), :]
+        down[2 * n : 3 * n] = prev_free[pl.ds(0, n, stride=sy), :]
+        down[3 * n : 3 * n + 5 * sx] = own[pl.ds(field, 5 * sx, stride=sy), :]
+
+    @pl.when(odd[0] == 1)
+    def _():
+        fill(message_b, message_a)
+
+    @pl.when(odd[0] == 0)
+    def _():
+        fill(message_a, message_b)
 
 
 def helpers(sizes, basis, stiff, op_high, op_low):
@@ -165,24 +173,69 @@
     return base, out_base, not_last, not_first, corner_tiles, weights, scaled, apply, node_parts
 
 
-def current_kernel(
-    sizes, place, own, prev_free, from_low, from_high,
-    pair_a, pair_b, corner_a, corner_b, op_high, op_low,
-    basis, applied, a_out, b_out, stiff_out, mass_out, share_out, stiff, lumped,
-    edge, stiff_edge, mass_rows, scale, above, below,
-):
+def element_layer(sizes, tools, edge, stiff_edge, mass_rows, stiff_out, mass_out, pair, layer):
+    cols, sx, sy, sz = sizes
+    _, _, not_last, _, corner_tiles, weights, scaled, apply, node_parts = tools
+
+    def edge_tiles(k, layer):
+        plain = stiff_edge[pl.ds((layer + 1) * SLAB, SLAB), :]
+        cut = plain * jnp.concatenate([not_last, not_last], 0)
+        tiles = []
+        for a in range(2):
+            tile = edge[pl.ds(((layer + 1 + a) * cols + k) * SLAB, SLAB), :]
+            tiles.append(tile * plain)
+            tiles.append(pltpu.roll(tile, sz - 1, 1) * cut)
+        return tiles
+
+    inner = 0 <= layer < sx
+    columns = []
+    kept = []
+    for c in range(2):
+        k = pair * 2 + c
+        tiles = corner_tiles(k, layer)
+        kept.append(tiles)
+        columns.append(jnp.concatenate(scaled(tiles, layer) + edge_tiles(k, layer), 0))
+    out, forces, doubled = apply(columns, NODE_ROWS + FORCE_ROWS if inner else NODE_ROWS, FORCE_ROWS + EDGE)
+    results = []
+    for c in range(2):
+        k = pair * 2 + c
+        if inner:
+            work = forces[:, c * sz : (c + 1) * sz] * doubled[:, c * sz : (c + 1) * sz]
+            energy = 0.0
+            square = [0.0, 0.0]
+            for alpha in range(24):
+                q = (alpha // 3) % 2
+                tile = kept[c][alpha]
+                energy = energy + work[alpha * sy : (alpha + 1) * sy]
+                square[q] = square[q] + tile * tile
+            at = (k * sx + layer) * sy
+            mass = mass_rows[pl.ds((layer + 1) * SLAB + 1, sy), :]
+            stiff_out[pl.ds(at, sy), :] = energy * (3.0 / weights(layer)[0])
+            mass_out[pl.ds(at, sy), :] = mass * (square[0] + square[1] * not_last)
+        results.append(node_parts(out[:, c * sz : (c + 1) * sz]))
+    return results
+
+
+def store_parts(sy, ref, k, result):
+    parts, rim = result
+    for i, tile in enumerate(parts + [rim]):
+        ref[pl.ds((k * 7 + i) * sy, sy), :] = tile
+
+
+def load_parts(sy, ref, k):
+    tiles = [ref[pl.ds((k * 7 + i) * sy, sy), :] for i in range(7)]
+    return tiles[0:6], tiles[6]
+
+
+def unpackers(sizes, tools, basis, edge, stiff, stiff_edge, mass_rows, scale):
     cols, sx, sy, sz = sizes
     slabs = cols * 3
     block = slabs * sx * sy
     plane = sx * sy
     field = block + slabs * sy
-    low_rows = from_low.shape[0]
     n = slabs * sx
     span = sy + 1
-
-    base, out_base, not_last, not_first, corner_tiles, weights, scaled, apply, node_parts = helpers(
-        sizes, basis, stiff, op_high, op_low
-    )
+    base = tools[0]
 
     def unpack(layer, source, low, high, at):
         low_ref, low_at = low
@@ -213,28 +266,72 @@
         mass_rows[pl.ds(index * SLAB + 1, sy), :] = source[pl.ds(field + plane + at * sy, sy), :]
         mass_rows[pl.ds(index * SLAB + 1 + sy, 1), :] = high_ref[pl.ds(high_at + 3 * n + sx + at, 1), :]
 
-    def unpack_nodes(layer, source, prev_source, high, at, prev_stride, prev_at):
+    def unpack_prev(layer, source, high, at, stride, start):
         high_ref, high_at = high
         for k in range(cols):
             for d in range(3):
-                basis[pl.ds(base(layer, 3 * cols + k, d), sy), :] = prev_source[
-                    pl.ds(prev_at + ((k * 3 + d) * prev_stride) * sy, sy), :
+                basis[pl.ds(base(layer, 3 * cols + k, d), sy), :] = source[
+                    pl.ds(start + ((k * 3 + d) * stride + at) * sy, sy), :
                 ]
         basis[pl.ds(base(layer, 3 * cols, 0) + sy, slabs, stride=span), :] = high_ref[
             pl.ds(high_at + 2 * n + at, slabs, stride=sx), :
         ]
+
+    def unpack_scale(layer, source, high, at):
+        high_ref, high_at = high
         for d in range(3):
             scale[pl.ds((layer * 3 + d) * SLAB, sy), :] = source[pl.ds(field + 2 * plane + (d * sx + at) * sy, sy), :]
         scale[pl.ds(layer * 3 * SLAB + sy, 3, stride=SLAB), :] = high_ref[pl.ds(high_at + 3 * n + 2 * sx + at, 3, stride=sx), :]
 
+    return unpack, unpack_fields, unpack_prev, unpack_scale
+
+
+def early_kernel(
+    sizes, own, prev_free, from_low, from_high, op_high, op_low,
+    basis, edge, stiff, stiff_edge, mass_rows, scale, stiff_out, mass_out, parts_out, prev_parts,
+):
+    cols, sx, sy, sz = sizes
+    tools = helpers(sizes, basis, stiff, op_high, op_low)
+    _, _, _, _, corner_tiles, _, scaled, apply, node_parts = tools
+    unpack, unpack_fields, unpack_prev, unpack_scale = unpackers(
+        sizes, tools, basis, edge, stiff, stiff_edge, mass_rows, scale
+    )
     edge[...] = jnp.zeros(edge.shape, f32)
     stiff_edge[...] = jnp.zeros(stiff_edge.shape, f32)
-    own_low = (from_low, 0)
-    own_high = (from_high, 0)
+    low = (from_low, 0)
+    high = (from_high, 0)
     for layer in range(sx):
-        unpack(layer, own, own_low, own_high, layer)
-        unpack_fields(layer, own, own_low, own_high, layer)
-        unpack_nodes(layer, own, prev_free, own_high, layer, sx, layer * sy)
+        unpack(layer, own, low, high, layer)
+        unpack_fields(layer, own, low, high, layer)
+        unpack_prev(layer, prev_free, high, layer, sx, 0)
+        unpack_scale(layer, own, high, layer)
+    for layer in range(sx - 1):
+        for pair in range(cols // 2):
+            results = element_layer(sizes, tools, edge, stiff_edge, mass_rows, stiff_out, mass_out, pair, layer)
+            for c in range(2):
+                store_parts(sy, parts_out, layer * cols + pair * 2 + c, results[c])
+        for pair in range(cols // 2):
+            ks = [3 * cols + pair * 2 + c for c in range(2)]
+            out = apply([jnp.concatenate(scaled(corner_tiles(k, layer), layer), 0) for k in ks], NODE_ROWS, FORCE_ROWS)[0]
+            for c in range(2):
+                store_parts(sy, prev_parts, layer * cols + pair * 2 + c, node_parts(out[:, c * sz : (c + 1) * sz]))
+
+
+def current_kernel(
+    sizes, place, pair_a, pair_b, corner_a, corner_b, op_high, op_low, parts_in,
+    basis_in, edge_in, stiff_in, stiff_edge_in, mass_in, scale_in, energy_in, square_in,
+    basis, edge, stiff, stiff_edge, mass_rows, scale, stiff_out, mass_out,
+    applied, a_out, b_out, share_out, lumped,
+    above, below,
+):
+    cols, sx, sy, sz = sizes
+    low_rows = -(-(cols * 3 * sx + 2 * sx) // 8) * 8
+    block = cols * 3 * sx * sy
+    tools = helpers(sizes, basis, stiff, op_high, op_low)
+    base, out_base, _, not_first, _, _, _, _, _ = tools
+    unpack, unpack_fields, unpack_prev, unpack_scale = unpackers(
+        sizes, tools, basis, edge, stiff, stiff_edge, mass_rows, scale
+    )
 
     def unpack_sides(lower, lower_corner, upper, upper_corner):
         lower_high = (lower_corner, low_rows)
@@ -244,7 +341,8 @@
         for step in range(2):
             unpack(sx + step, upper, (upper_corner, 0), upper_high, step)
         unpack_fields(sx, upper, (upper_corner, 0), upper_high, 0)
-        unpack_nodes(sx, upper, upper, upper_high, 0, 1, block)
+        unpack_prev(sx, upper, upper_high, 0, 1, block)
+        unpack_scale(sx, upper, upper_high, 0)
 
     @pl.when(place[0] == 1)
     def _():
@@ -266,49 +364,20 @@
         outer = outer + pltpu.roll(outer, 1, 1) * not_first
         lumped[pl.ds(layer * SLAB + sy, 1), :] = outer[0:1]
 
-    def edge_tiles(k, layer):
-        plain = stiff_edge[pl.ds((layer + 1) * SLAB, SLAB), :]
-        cut = plain * jnp.concatenate([not_last, not_last], 0)
-        tiles = []
-        for a in range(2):
-            tile = edge[pl.ds(((layer + 1 + a) * cols + k) * SLAB, SLAB), :]
-            tiles.append(tile * plain)
-            tiles.append(pltpu.roll(tile, sz - 1, 1) * cut)
-        return tiles
-
     above[...] = jnp.zeros(above.shape, f32)
     below[...] = jnp.zeros(below.shape, f32)
 
-    def current_pair(pair, carry):
+    def current_pair(pair):
         sums = [[0.0, 0.0], [0.0, 0.0]]
         tails = [None, None]
         for layer in range(-1, sx + 1):
-            inner = 0 <= layer < sx
-            columns = []
-            kept = []
+            if 0 <= layer < sx - 1:
+                results = [load_parts(sy, parts_in, layer * cols + pair * 2 + c) for c in range(2)]
+            else:
+                results = element_layer(sizes, tools, edge, stiff_edge, mass_rows, stiff_out, mass_out, pair, layer)
             for c in range(2):
                 k = pair * 2 + c
-                tiles = corner_tiles(k, layer)
-                kept.append(tiles)
-                columns.append(jnp.concatenate(scaled(tiles, layer) + edge_tiles(k, layer), 0))
-            out, forces, doubled = apply(columns, NODE_ROWS + FORCE_ROWS if inner else NODE_ROWS, FORCE_ROWS + EDGE)
-            for c in range(2):
-                k = pair * 2 + c
-                part = out[:, c * sz : (c + 1) * sz]
-                if inner:
-                    work = forces[:, c * sz : (c + 1) * sz] * doubled[:, c * sz : (c + 1) * sz]
-                    energy = 0.0
-                    square = [0.0, 0.0]
-                    for alpha in range(24):
-                        q = (alpha // 3) % 2
-                        tile = kept[c][alpha]
-                        energy = energy + work[alpha * sy : (alpha + 1) * sy]
-                        square[q] = square[q] + tile * tile
-                    at = (k * sx + layer) * sy
-                    mass = mass_rows[pl.ds((layer + 1) * SLAB + 1, sy), :]
-                    stiff_out[pl.ds(at, sy), :] = energy * (3.0 / weights(layer)[0])
-                    mass_out[pl.ds(at, sy), :] = mass * (square[0] + square[1] * not_last)
-                parts, rim = node_parts(part)
+                parts, rim = results[c]
                 if layer >= 0:
                     before, rim_before = tails[c]
                     rim_sum = rim[0:3] + rim_before[3:6]
@@ -339,9 +408,9 @@
         for c in range(2):
             above[pl.ds(pair * 2 + c, 1), :] = jnp.sum(sums[c][0], 0, keepdims=True)
             below[pl.ds(pair * 2 + c, 1), :] = jnp.sum(sums[c][1], 0, keepdims=True)
-        return carry
-
-    lax.fori_loop(0, cols // 2, current_pair, 0, unroll=cols // 2)
+
+    for pair in range(cols // 2):
+        current_pair(pair)
 
     half = sz // 2
     rows = cols * sx * sy
@@ -358,23 +427,25 @@
     share_out[rows:] = jnp.where(spot == OTHER_TOP, top, 0.0) + jnp.where(spot == OTHER_TOP + 1, bottom, 0.0)
 
 
-def gram_kernel(sizes, basis, stiff, lumped, op_high, op_low, applied_in, applied, gram_out):
+def gram_kernel(sizes, basis, stiff, lumped, op_high, op_low, prev_parts, applied_in, applied, gram_out):
     cols, sx, sy, sz = sizes
     width = 4 * cols
     span = sy + 1
-    base, out_base, _, _, corner_tiles, _, scaled, apply, node_parts = helpers(sizes, basis, stiff, op_high, op_low)
-
-    def other_pair(pair, carry):
+    _, out_base, _, _, corner_tiles, _, scaled, apply, node_parts = helpers(sizes, basis, stiff, op_high, op_low)
+
+    def other_pair(pair):
         tails = [None, None]
         for layer in range(sx):
-            columns = []
+            first = cols + pair * 2
+            if first >= 3 * cols and layer < sx - 1:
+                results = [load_parts(sy, prev_parts, layer * cols + first - 3 * cols + c) for c in range(2)]
+            else:
+                columns = [jnp.concatenate(scaled(corner_tiles(first + c, layer), layer), 0) for c in range(2)]
+                out = apply(columns, NODE_ROWS, FORCE_ROWS)[0]
+                results = [node_parts(out[:, c * sz : (c + 1) * sz]) for c in range(2)]
             for c in range(2):
-                k = cols + pair * 2 + c
-                columns.append(jnp.concatenate(scaled(corner_tiles(k, layer), layer), 0))
-            out = apply(columns, NODE_ROWS, FORCE_ROWS)[0]
-            for c in range(2):
-                k = cols + pair * 2 + c
-                parts, rim = node_parts(out[:, c * sz : (c + 1) * sz])
+                k = first + c
+                parts, rim = results[c]
                 ends = [(layer, parts[0:3], rim[0:3], tails[c])]
                 if layer == sx - 1:
                     ends.append((sx, parts[3:6], rim[3:6], None))
@@ -388,9 +459,9 @@
                         applied[pl.ds(out_base(at, k, d), sy), :] = value
                         applied[pl.ds(out_base(at, k, d) + sy, 1), :] = last
                 tails[c] = (parts, rim)
-        return carry
-
-    lax.fori_loop(0, 3 * cols // 2, other_pair, 0, unroll=3 * cols // 2)
+
+    for pair in range(3 * cols // 2):
+        other_pair(pair)
 
     def contract(left, right):
         return lax.dot_general(left, right, (((1,), (1,)), ((), ())), preferred_element_type=f32)
@@ -404,36 +475,22 @@
         both = contract(jnp.concatenate([left_high, left_low], 0), right_high)
         return both[0:rows] + both[rows:] + contract(left_high, right_low)
 
-    def gram_group(index, carry):
-        layer = index // 3
-        d = index - layer * 3
-        values = []
-        others = []
-        for y in range(sy):
-            value = basis[pl.ds(((layer + 1) * width * 3 + d) * span + y, width, stride=step), :]
-            other = applied[pl.ds((layer * width * 3 + d) * span + y, width, stride=step), :]
-            values.append(value)
-            others.append(jnp.concatenate([other, value * lumped[pl.ds(layer * SLAB + y, 1), :]], 0))
-        return carry + product(others, values)
-
-    both = lax.fori_loop(0, 3 * sx, gram_group, jnp.zeros((width, 2 * width), f32))
-
-    def gram_end(d, carry):
-        values = []
-        others = []
-        for y in range(sy):
-            values.append(basis[pl.ds(((sx + 1) * width * 3 + d) * span + y, width, stride=step), :])
-            others.append(applied[pl.ds((sx * width * 3 + d) * span + y, width, stride=step), :])
-        return carry + product(others, values)
-
-    gram_stiff = lax.fori_loop(0, 3, gram_end, both[:, 0:width])
-    values = []
-    others = []
-    for layer in range(sx + 1):
+    def gram_layer(layer, carry):
+        counted = (layer < sx).astype(f32)
         for d in range(3):
-            values.append(basis[pl.ds(base(layer, 0, d) + sy, width, stride=step), :])
-            others.append(applied[pl.ds(out_base(layer, 0, d) + sy, width, stride=step), :])
-    gram_stiff = gram_stiff + product(others, values)
+            values = []
+            others = []
+            for y in range(sy + 1):
+                value = basis[pl.ds(((layer + 1) * width * 3 + d) * span + y, width, stride=step), :]
+                other = applied[pl.ds((layer * width * 3 + d) * span + y, width, stride=step), :]
+                mass = lumped[pl.ds(layer * SLAB + y, 1), :] * counted
+                values.append(value)
+                others.append(jnp.concatenate([other, value * mass if y < sy else jnp.zeros_like(value)], 0))
+            carry = carry + product(others, values)
+        return carry
+
+    both = lax.fori_loop(0, sx + 1, gram_layer, jnp.zeros((width, 2 * width), f32))
+    gram_stiff = both[:, 0:width]
     gram_out[...] = jnp.zeros(gram_out.shape, f32)
     gram_out[:, 0:width] = gram_stiff
     gram_out[:, 64 : 64 + width] = both[:, width : 2 * width]
@@ -492,11 +549,6 @@
     sensitivity[...] = total[:, 0:half].reshape(sx, sy, half)
 
 
-def line(axis, step):
-    count = lax.axis_size(axis)
-    return [(i, i + step) for i in range(count) if 0 <= i + step < count]
-
-
 def pairs(axis, first):
     count = lax.axis_size(axis)
     steps = []
@@ -543,16 +595,19 @@
     up_rows = -(-(n + 2 * sx) // 8) * 8
     down_rows = -(-(3 * n + 5 * sx) // 8) * 8
     sources = (current, previous, modulus, density, solid, preconditioner, clamped)
-    own, prev_free, up, down = pl.pallas_call(
+    odd_y = (lax.axis_index("by") % 2).astype(jnp.int32)
+    own, prev_free, message_a, message_b = pl.pallas_call(
         lambda *refs: prepare_kernel(sizes, *refs),
-        in_specs=[pl.BlockSpec(memory_space=pltpu.HBM)] * len(sources),
+        in_specs=[pl.BlockSpec(memory_space=pltpu.SMEM)] + [pl.BlockSpec(memory_space=pltpu.HBM)] * len(sources),
         scratch_shapes=[pltpu.VMEM(x.shape, x.dtype) for x in sources] + [pltpu.SemaphoreType.DMA((len(sources),))],
-        out_shape=(kept(own_rows, sz), kept(block, sz), kept(up_rows, sz), kept(down_rows, sz)),
+        out_shape=(kept(own_rows, sz), kept(block, sz), kept(down_rows, sz), kept(down_rows, sz)),
         compiler_params=pltpu.CompilerParams(vmem_limit_bytes=12 << 20),
         name="prepare",
-    )(*[far(x) for x in sources])
-    from_low = lax.ppermute(up, "by", line("by", 1))
-    from_high = lax.ppermute(down, "by", line("by", -1))
+    )(odd_y.reshape(1), *[far(x) for x in sources])
+    rows_a = lax.ppermute(message_a, "by", pairs("by", 0))
+    rows_b = lax.ppermute(message_b, "by", pairs("by", 1))
+    from_low = jnp.where(odd_y == 1, rows_a[:up_rows], rows_b[:up_rows])
+    from_high = jnp.where(odd_y == 1, rows_b, rows_a)
     row_pick, col_pick, op_mask = operator_tables(sy)
     tables = (element_stiffness, jnp.asarray(row_pick, bf16), jnp.asarray(col_pick, bf16), jnp.asarray(op_mask, bf16))
     op_high, op_low = pl.pallas_call(
@@ -565,7 +620,6 @@
     )(*[far(x) for x in tables])
     pair_a = lax.ppermute(own, "bx", pairs("bx", 0))
     pair_b = lax.ppermute(own, "bx", pairs("bx", 1))
-    from_low, from_high, op_high, op_low = lax.optimization_barrier((from_low, from_high, op_high, op_low))
     corner = jnp.concatenate([from_low, from_high], 0)
     corner_a = lax.ppermute(corner, "bx", pairs("bx", 0))
     corner_b = lax.ppermute(corner, "bx", pairs("bx", 1))
@@ -575,41 +629,51 @@
     energies = cols * sx * sy
     vmem = pl.BlockSpec(memory_space=pltpu.VMEM)
     smem = pl.BlockSpec(memory_space=pltpu.SMEM)
-    basis, applied, a_part, b_part, stiff_part, mass_part, shared, stiff, lumped = pl.pallas_call(
+    low_limit = pltpu.CompilerParams(vmem_limit_bytes=16 << 20)
+    state_shapes = (
+        kept((sx + 3) * width * 3 * span, sz),
+        kept((sx + 3) * cols * SLAB, sz),
+        kept((sx + 2) * sy, sz),
+        kept((sx + 2) * SLAB, sz),
+        kept((sx + 2) * SLAB, sz),
+        kept((sx + 1) * 3 * SLAB, sz),
+        kept(energies, sz),
+        kept(energies, sz),
+    )
+    parts_shape = kept((sx - 1) * cols * 7 * sy, sz)
+    *state, parts, prev_parts = pl.pallas_call(
+        lambda *refs: early_kernel(sizes, *refs),
+        in_specs=[vmem] * 6,
+        out_shape=state_shapes + (parts_shape, parts_shape),
+        compiler_params=low_limit,
+        name="early",
+    )(*[near(x) for x in (own, prev_free, from_low, from_high, op_high, op_low)])
+    basis, _, stiff, _, _, _, stiff_part, mass_part, applied, a_part, b_part, shared, lumped = pl.pallas_call(
         lambda *refs: current_kernel(sizes, *refs),
-        in_specs=[smem] + [vmem] * 10,
-        out_shape=(
-            kept((sx + 3) * width * 3 * span, sz),
+        in_specs=[smem] + [vmem] * 15,
+        out_shape=state_shapes
+        + (
             kept((sx + 1) * width * 3 * span, sz),
             kept(block, sz),
             kept(block, sz),
-            kept(energies, sz),
-            kept(energies, sz),
             kept(energies + 16, sz),
-            kept((sx + 2) * sy, sz),
             kept((sx + 1) * SLAB, sz),
         ),
-        scratch_shapes=[
-            pltpu.VMEM(((sx + 3) * cols * SLAB, sz), f32),
-            pltpu.VMEM(((sx + 2) * SLAB, sz), f32),
-            pltpu.VMEM(((sx + 2) * SLAB, sz), f32),
-            pltpu.VMEM(((sx + 1) * 3 * SLAB, sz), f32),
-            pltpu.VMEM((16, sz), f32),
-            pltpu.VMEM((16, sz), f32),
-        ],
-        compiler_params=pltpu.CompilerParams(vmem_limit_bytes=16 << 20),
+        input_output_aliases={8 + i: i for i in range(8)},
+        scratch_shapes=[pltpu.VMEM((16, sz), f32), pltpu.VMEM((16, sz), f32)],
+        compiler_params=low_limit,
         name="current",
-    )(place, *[near(x) for x in (own, prev_free, from_low, from_high, pair_a, pair_b, corner_a, corner_b, op_high, op_low)])
+    )(place, *[near(x) for x in (pair_a, pair_b, corner_a, corner_b, op_high, op_low, parts, *state)])
     count = lax.axis_size("real")
     other = lax.ppermute(shared, "real", [(i, (i + 1) % count) for i in range(count)])
     _, gram = pl.pallas_call(
         lambda *refs: gram_kernel(sizes, *refs),
-        in_specs=[vmem] * 6,
+        in_specs=[vmem] * 7,
         out_shape=(kept((sx + 1) * width * 3 * span, sz), kept(width, 128)),
-        input_output_aliases={5: 0},
+        input_output_aliases={6: 0},
         compiler_params=pltpu.CompilerParams(vmem_limit_bytes=16 << 20),
         name="gram",
-    )(*[near(x) for x in (basis, stiff, lumped, op_high, op_low, applied)])
+    )(*[near(x) for x in (basis, stiff, lumped, op_high, op_low, prev_parts, applied)])
     gram = jnp.concatenate([gram[0:16] + other[energies:], gram[16:]], 0)
     gram = sum_over(sum_over(gram, "bx"), "by")
     stiff_gram, mass_gram, search, sensitivity = pl.pallas_call(

time: 45.9 us -> 43.3 us (0.943)
  waiting for transfers between devices: 9.2 us -> 7.28 us
  starting transfers between devices: 22.5 us -> 22 us
    ppermute x4, starting transfers between devices: 8.09 us -> 10.3 us  [sum_over(): lax.ppermute(value, axis, [(i, i ^ distance) for i in range(count)])]
    ppermute x2, starting transfers between devices: 5.83 us -> 3.77 us  [the longest x1 3.11 us: shards(): rows_a = lax.ppermute(message_a, 'by', pairs('by', 0))]
    ppermute x1, starting transfers between devices: 4.39 us -> 2.92 us  [shards(): pair_a = lax.ppermute(own, 'bx', pairs('bx', 0))]
    pallas_call x0 -> x1, Pallas kernels: none -> 1.47 us  [shards(): pl.pallas_call(lambda *refs: early_kernel(sizes, *refs), in_specs=[vmem]...]
    pallas_call x1, Pallas kernels: 4.84 us -> 3.81 us  [shards(): pl.pallas_call(lambda *refs: gram_kernel(sizes, *refs), in_specs=[vmem] *...]
    ppermute x4, waiting for transfers between devices: 8.24 us -> 7.26 us  [sum_over(): lax.ppermute(value, axis, [(i, i ^ distance) for i in range(count)])]
    ppermute x1, waiting for transfers between devices: 0.94 us -> 0.01 us  [shards(): corner_a = lax.ppermute(corner, 'bx', pairs('bx', 0))]
    ppermute x1, starting transfers between devices: 1.34 us -> 2.06 us  [shards(): corner_a = lax.ppermute(corner, 'bx', pairs('bx', 0))]
  transfers between devices with their start and end apart: 11 -> 11, of which waited for: 5 -> 4; matrix products, arithmetic and copies ran while one was open for 0% -> 0% of each run, Pallas kernels for 14% -> 16%
where the time goes in v1:
time: 43.3 us; the launch traced here: 43 us
  starting transfers between devices  22 us (51%)
  Pallas kernels  12.9 us (30%)
  waiting for transfers between devices  7.28 us (17%)
  between operations  0.77 us (2%)
    ppermute x4, starting transfers between devices, sum_over(): lax.ppermute(value, axis, [(i, i ^ distance) for i in range(count)])  10.3 us
    ppermute x4, waiting for transfers between devices, sum_over(): lax.ppermute(value, axis, [(i, i ^ distance) for i in range(count)])  7.26 us
    pallas_call x1, Pallas kernels, shards(): pl.pallas_call(lambda *refs: gram_kernel(sizes, *refs), in_specs=[vmem] *...  3.81 us
    ppermute x1, starting transfers between devices, shards(): rows_a = lax.ppermute(message_a, 'by', pairs('by', 0))  3.11 us
    ppermute x1, starting transfers between devices, shards(): pair_a = lax.ppermute(own, 'bx', pairs('bx', 0))  2.92 us
    pallas_call x1, Pallas kernels, shards(): pl.pallas_call(lambda *refs: current_kernel(sizes, *refs), in_specs=[smem...  2.87 us
    ppermute x1, starting transfers between devices, shards(): corner_a = lax.ppermute(corner, 'bx', pairs('bx', 0))  2.06 us
    pallas_call x1, Pallas kernels, shards(): pl.pallas_call(lambda *refs: finish_kernel(sizes, dof, *refs), in_specs=[...  1.76 us
  transfers between devices with their start and end apart: 11, of which 4 were waited for; matrix products, arithmetic and copies ran while one was open for 0% of the time, Pallas kernels for 16%

profile of v1, /device:TPU:0, one launch (start us, length us, event | category | flops | bytes accessed | tf_op | source)
XLA Modules:
  0.0 43.0 jit_solution(1736091711501679457)
XLA Ops:
  0.6 1.3 %prepare.1 = (f32[944,128]{1,0:T(8,128)S(1)}, f32[576,128]{1,0:T(8,128)S(1)}, f32[232,128]{1,0:T(8,128)S(1)}, f32[232,128]{1,0:T(8,128)S(1)}) custom-call(s32[1]{0:T(128)} %bitcast.2.refs_0_, f32[1,12,3,2,8,128]{5,4,3,2,1,0:T(8,128)} %refs_1_.2, f32[1,12,3,2,8,128]{5,4,3,2,1,0:T(8,128)} %refs_2_.2, f32[2,8,128]{2,1,0:T(8,128)} %refs_3_.2, ...), custom_call_target="tpu_custom_call" | custom-call | tf_op jit(solution)/shard_map/prepare/pallas_call | solution.py:599
  1.9 3.1 %collective-permute-start.2 = (f32[232,128]{1,0:T(8,128)S(1)}, f32[232,128]{1,0:T(8,128)S(1)}, u32[]{:S(2)}, u32[]{:S(2)}) collective-permute-start(f32[232,128]{1,0:T(8,128)S(1)} %get-tuple-element.35), channel_id=1, source_target_pairs={{0,1},{1,0},{2,3},{3,2},{4,5},{5,4},{6,7},{7,6},{8,9},{9,8},{10,11... | collective-permute-start | bytes 356360 | tf_op jit(solution)/shard_map/ppermute | solution.py:607
  5.0 0.7 %collective-permute-start.3 = (f32[232,128]{1,0:T(8,128)S(1)}, f32[232,128]{1,0:T(8,128)S(1)}, u32[]{:S(2)}, u32[]{:S(2)}) collective-permute-start(f32[232,128]{1,0:T(8,128)S(1)} %get-tuple-element.36), channel_id=1, source_target_pairs={{1,2},{2,1},{5,6},{6,5},{9,10},{10,9},{13,14},{14,13},{17,18},{18,... | collective-permute-start | bytes 356360 | tf_op jit(solution)/shard_map/ppermute | solution.py:608
  5.7 0.7 %collective-permute-start.1 = (f32[944,128]{1,0:T(8,128)S(1)}, f32[944,128]{1,0:T(8,128)S(1)}, u32[]{:S(2)}, u32[]{:S(2)}) collective-permute-start(f32[944,128]{1,0:T(8,128)S(1)} %get-tuple-element.34.refs_0_), channel_id=1, source_target_pairs={{4,8},{8,4},{5,9},{9,5},{6,10},{10,6},{7,11},{11,7},{20,24},{24,20... | collective-permute-start | bytes 1449992 | tf_op jit(solution)/shard_map/ppermute | solution.py:622
  6.4 2.9 %collective-permute-start = (f32[944,128]{1,0:T(8,128)S(1)}, f32[944,128]{1,0:T(8,128)S(1)}, u32[]{:S(2)}, u32[]{:S(2)}) collective-permute-start(f32[944,128]{1,0:T(8,128)S(1)} %get-tuple-element.34.refs_0_), channel_id=1, source_target_pairs={{0,4},{4,0},{8,12},{12,8},{1,5},{5,1},{9,13},{13,9},{2,6},{6,2},{1... | collective-permute-start | bytes 1449992 | tf_op jit(solution)/shard_map/ppermute | solution.py:621
  9.4 0.7 %collective-permute-start.5 = (f32[312,128]{1,0:T(8,128)S(1)}, f32[312,128]{1,0:T(8,128)S(1)}, u32[]{:S(2)}, u32[]{:S(2)}) collective-permute-start(f32[312,128]{1,0:T(8,128)S(1)} %pad_maximum_fusion), channel_id=1, source_target_pairs={{4,8},{8,4},{5,9},{9,5},{6,10},{10,6},{7,11},{11,7},{20,24},{24,20... | collective-permute-start | bytes 479240 | tf_op jit(solution)/shard_map/ppermute | solution.py:625
  10.1 2.1 %collective-permute-start.4 = (f32[312,128]{1,0:T(8,128)S(1)}, f32[312,128]{1,0:T(8,128)S(1)}, u32[]{:S(2)}, u32[]{:S(2)}) collective-permute-start(f32[312,128]{1,0:T(8,128)S(1)} %pad_maximum_fusion), channel_id=1, source_target_pairs={{0,4},{4,0},{8,12},{12,8},{1,5},{5,1},{9,13},{13,9},{2,6},{6,2},{1... | collective-permute-start | bytes 479240 | tf_op jit(solution)/shard_map/ppermute | solution.py:624
  12.1 1.7 %operator.1 = (bf16[304,256]{1,0:T(8,128)(2,1)S(1)}, bf16[304,256]{1,0:T(8,128)(2,1)S(1)}) custom-call(f32[24,24]{1,0:T(8,128)} %refs_0_.1, bf16[2,304,24]{2,1,0:T(8,128)(2,1)} %constant.37.clone.refs_1_, bf16[24,256]{1,0:T(8,128)(2,1)} %constant.38.clone.refs_2_, bf16[2,304,256]{2,1,0:T(8,128)(2,1)} %constant.39.clone.refs_3_), custom_call_target="tpu_custom_call" | custom-call | tf_op jit(solution)/shard_map/operator/pallas_call | solution.py:613
  13.8 0.1 pad_add_fusion.refs_0_
  13.9 1.5 %early.1 = (f32[6480,128]{1,0:T(8,128)S(1)}, f32[960,128]{1,0:T(8,128)S(1)}, f32[32,128]{1,0:T(8,128)S(1)}, f32[64,128]{1,0:T(8,128)S(1)}, f32[64,128]{1,0:T(8,1...) custom-call(f32[944,128]{1,0:T(8,128)S(1)} %get-tuple-element.34.ref, ...), custom_call_target="tpu_custom_call" | custom-call | tf_op jit(solution)/shard_map/early/pallas_call | solution.py:644
  15.4 0.0 collective-permute-done.4.refs_3_
  15.4 0.0 collective-permute-done.1.refs_2_
  15.4 2.9 %current.1 = (f32[6480,128]{1,0:T(8,128)S(1)}, f32[960,128]{1,0:T(8,128)S(1)}, f32[32,128]{1,0:T(8,128)S(1)}, f32[64,128]{1,0:T(8,128)S(1)}, f32[64,128]{1,0:T(8...) custom-call(s32[2]{0:T(128)S(1)} %pad_add_fusion.refs_0_, ...), custom_call_target="tpu_custom_call", output_to_operand_aliasing={{0}: (8, {}), {1}: (9, {}), {2}: (10, {}), {3}: (11, {}), {... | custom-call | tf_op jit(solution)/shard_map/current/pallas_call | solution.py:651
  18.3 1.5 %collective-permute-start.6 = (f32[208,128]{1,0:T(8,128)S(1)}, f32[208,128]{1,0:T(8,128)S(1)}, u32[]{:S(2)}, u32[]{:S(2)}) collective-permute-start(f32[208,128]{1,0:T(8,128)S(1)} %get-tuple-element.55), channel_id=1, source_target_pairs={{0,16},{16,0},{1,17},{17,1},{2,18},{18,2},{3,19},{19,3},{4,20},{20... | collective-permute-start | bytes 319496 | tf_op jit(solution)/shard_map/ppermute | solution.py:668
  19.8 3.8 %gram.1 = (f32[3888,128]{1,0:T(8,128)S(1)}, f32[48,128]{1,0:T(8,128)S(1)}) custom-call(f32[6480,128]{1,0:T(8,128)S(1)} %get-tuple-element.49.refs_0_, f32[32,128]{1,0:T(8,128)S(1)} %get-tuple-element.50.refs_1_, f32[48,128]{1,0:T(8,128)S(1)} %get-tuple-element.51.refs_2_, ...), custom_call_target="tpu_custom_call", output_to_operand_aliasing={{0}: (6, {})} | custom-call | tf_op jit(solution)/shard_map/gram/pallas_call | solution.py:669
  23.6 1.8 %collective-permute-start.7 = (f32[48,128]{1,0:T(8,128)S(1)}, f32[48,128]{1,0:T(8,128)S(1)}, u32[]{:S(2)}, u32[]{:S(2)}) collective-permute-start(f32[48,128]{1,0:T(8,128)S(1)} %pad_maximum_fusion.1), channel_id=1, source_target_pairs={{0,4},{4,0},{8,12},{12,8},{1,5},{5,1},{9,13},{13,9},{2,6},{6,2},{1... | collective-permute-start | bytes 73736 | tf_op jit(solution)/shard_map/ppermute | solution.py:566
  25.4 0.8 %collective-permute-done.7 = f32[48,128]{1,0:T(8,128)S(1)} collective-permute-done((f32[48,128]{1,0:T(8,128)S(1)}, f32[48,128]{1,0:T(8,128)S(1)}, u32[]{:S(2)}, u32[]{:S(2)}) %collective-permute-start.7) | collective-permute-done | bytes 24608 | tf_op jit(solution)/shard_map/ppermute | solution.py:566
  26.3 2.2 %collective-permute-start.8 = (f32[48,128]{1,0:T(8,128)S(1)}, f32[48,128]{1,0:T(8,128)S(1)}, u32[]{:S(2)}, u32[]{:S(2)}) collective-permute-start(f32[48,128]{1,0:T(8,128)S(1)} %fusion), channel_id=1, source_target_pairs={{0,8},{4,12},{8,0},{12,4},{1,9},{5,13},{9,1},{13,5},{2,10},{6,14},... | collective-permute-start | bytes 73736 | tf_op jit(solution)/shard_map/ppermute | solution.py:566
  28.5 1.8 %collective-permute-done.8 = f32[48,128]{1,0:T(8,128)S(1)} collective-permute-done((f32[48,128]{1,0:T(8,128)S(1)}, f32[48,128]{1,0:T(8,128)S(1)}, u32[]{:S(2)}, u32[]{:S(2)}) %collective-permute-start.8) | collective-permute-done | bytes 24608 | tf_op jit(solution)/shard_map/ppermute | solution.py:566
  30.3 4.4 %collective-permute-start.9 = (f32[48,128]{1,0:T(8,128)S(1)}, f32[48,128]{1,0:T(8,128)S(1)}, u32[]{:S(2)}, u32[]{:S(2)}) collective-permute-start(f32[48,128]{1,0:T(8,128)S(1)} %add.26), channel_id=1, source_target_pairs={{0,1},{1,0},{2,3},{3,2},{4,5},{5,4},{6,7},{7,6},{8,9},{9,8},{10,11... | collective-permute-start | bytes 73736 | tf_op jit(solution)/shard_map/ppermute | solution.py:566
  34.7 1.8 %collective-permute-done.9 = f32[48,128]{1,0:T(8,128)S(1)} collective-permute-done((f32[48,128]{1,0:T(8,128)S(1)}, f32[48,128]{1,0:T(8,128)S(1)}, u32[]{:S(2)}, u32[]{:S(2)}) %collective-permute-start.9) | collective-permute-done | bytes 24608 | tf_op jit(solution)/shard_map/ppermute | solution.py:566
  36.5 1.9 %collective-permute-start.10 = (f32[48,128]{1,0:T(8,128)S(1)}, f32[48,128]{1,0:T(8,128)S(1)}, u32[]{:S(2)}, u32[]{:S(2)}) collective-permute-start(f32[48,128]{1,0:T(8,128)S(1)} %add.27), channel_id=1, source_target_pairs={{0,2},{1,3},{2,0},{3,1},{4,6},{5,7},{6,4},{7,5},{8,10},{9,11},{10,... | collective-permute-start | bytes 73736 | tf_op jit(solution)/shard_map/ppermute | solution.py:566
  38.5 2.8 %collective-permute-done.10 = f32[48,128]{1,0:T(8,128)S(1)} collective-permute-done((f32[48,128]{1,0:T(8,128)S(1)}, f32[48,128]{1,0:T(8,128)S(1)}, u32[]{:S(2)}, u32[]{:S(2)}) %collective-permute-start.10) | collective-permute-done | bytes 24608 | tf_op jit(solution)/shard_map/ppermute | solution.py:566
  41.3 1.8 %finish.1 = (f32[36,1,36]{2,1,0:T(1,128)}, f32[36,1,36]{2,1,0:T(1,128)}, f32[1,12,3,2,8,128]{5,4,3,2,1,0:T(8,128)}, f32[2,8,64]{2,1,0:T(8,128)}) custom-call(s32[2]{0:T(128)S(1)} %pad_add_fusion.refs_0_, f32[48,128]{1,0:T(8,128)S(1)} %add.28.refs_1_, f32[576,128]{1,0:T(8,128)S(1)} %get-tuple-element.56.refs_2_, f32[576,128]{1,0:T(8,128)S(1)} %get-tuple-element.57.refs_3_, ...), custom_call_target="tpu_custom_call" | custom-call | tf_op jit(solution)/shard_map/finish/pallas_call | solution.py:679
  (15 shorter events, 0.1 us)
Async XLA Ops:
  1.9 7.4 %collective-permute-start.2 = (f32[232,128]{1,0:T(8,128)S(1)}, f32[232,128]{1,0:T(8,128)S(1)}, u32[]{:S(2)}, u32[]{:S(2)}) collective-permute-start(f32[232,128]{1,0:T(8,128)S(1)} %get-tuple-element.35), channel_id=1, source_target_pairs={{0,1},{1,0},{2,3},{3,2},{4,5},{5,4},{6,7},{7,6},{8,9},{9,8},{10,11... | collective-permute-start | bytes 356360 | tf_op jit(solution)/shard_map/ppermute | solution.py:607
  5.0 4.3 %collective-permute-start.3 = (f32[232,128]{1,0:T(8,128)S(1)}, f32[232,128]{1,0:T(8,128)S(1)}, u32[]{:S(2)}, u32[]{:S(2)}) collective-permute-start(f32[232,128]{1,0:T(8,128)S(1)} %get-tuple-element.36), channel_id=1, source_target_pairs={{1,2},{2,1},{5,6},{6,5},{9,10},{10,9},{13,14},{14,13},{17,18},{18,... | collective-permute-start | bytes 356360 | tf_op jit(solution)/shard_map/ppermute | solution.py:608
  5.7 9.7 %collective-permute-start.1 = (f32[944,128]{1,0:T(8,128)S(1)}, f32[944,128]{1,0:T(8,128)S(1)}, u32[]{:S(2)}, u32[]{:S(2)}) collective-permute-start(f32[944,128]{1,0:T(8,128)S(1)} %get-tuple-element.34.refs_0_), channel_id=1, source_target_pairs={{4,8},{8,4},{5,9},{9,5},{6,10},{10,6},{7,11},{11,7},{20,24},{24,20... | collective-permute-start | bytes 1449992 | tf_op jit(solution)/shard_map/ppermute | solution.py:622
  6.4 9.0 %collective-permute-start = (f32[944,128]{1,0:T(8,128)S(1)}, f32[944,128]{1,0:T(8,128)S(1)}, u32[]{:S(2)}, u32[]{:S(2)}) collective-permute-start(f32[944,128]{1,0:T(8,128)S(1)} %get-tuple-element.34.refs_0_), channel_id=1, source_target_pairs={{0,4},{4,0},{8,12},{12,8},{1,5},{5,1},{9,13},{13,9},{2,6},{6,2},{1... | collective-permute-start | bytes 1449992 | tf_op jit(solution)/shard_map/ppermute | solution.py:621
  9.4 6.0 %collective-permute-start.5 = (f32[312,128]{1,0:T(8,128)S(1)}, f32[312,128]{1,0:T(8,128)S(1)}, u32[]{:S(2)}, u32[]{:S(2)}) collective-permute-start(f32[312,128]{1,0:T(8,128)S(1)} %pad_maximum_fusion), channel_id=1, source_target_pairs={{4,8},{8,4},{5,9},{9,5},{6,10},{10,6},{7,11},{11,7},{20,24},{24,20... | collective-permute-start | bytes 479240 | tf_op jit(solution)/shard_map/ppermute | solution.py:625
  10.1 5.3 %collective-permute-start.4 = (f32[312,128]{1,0:T(8,128)S(1)}, f32[312,128]{1,0:T(8,128)S(1)}, u32[]{:S(2)}, u32[]{:S(2)}) collective-permute-start(f32[312,128]{1,0:T(8,128)S(1)} %pad_maximum_fusion), channel_id=1, source_target_pairs={{0,4},{4,0},{8,12},{12,8},{1,5},{5,1},{9,13},{13,9},{2,6},{6,2},{1... | collective-permute-start | bytes 479240 | tf_op jit(solution)/shard_map/ppermute | solution.py:624
  18.3 5.3 %collective-permute-start.6 = (f32[208,128]{1,0:T(8,128)S(1)}, f32[208,128]{1,0:T(8,128)S(1)}, u32[]{:S(2)}, u32[]{:S(2)}) collective-permute-start(f32[208,128]{1,0:T(8,128)S(1)} %get-tuple-element.55), channel_id=1, source_target_pairs={{0,16},{16,0},{1,17},{17,1},{2,18},{18,2},{3,19},{19,3},{4,20},{20... | collective-permute-start | bytes 319496 | tf_op jit(solution)/shard_map/ppermute | solution.py:668
  23.6 2.6 %collective-permute-start.7 = (f32[48,128]{1,0:T(8,128)S(1)}, f32[48,128]{1,0:T(8,128)S(1)}, u32[]{:S(2)}, u32[]{:S(2)}) collective-permute-start(f32[48,128]{1,0:T(8,128)S(1)} %pad_maximum_fusion.1), channel_id=1, source_target_pairs={{0,4},{4,0},{8,12},{12,8},{1,5},{5,1},{9,13},{13,9},{2,6},{6,2},{1... | collective-permute-start | bytes 73736 | tf_op jit(solution)/shard_map/ppermute | solution.py:566
  26.3 4.1 %collective-permute-start.8 = (f32[48,128]{1,0:T(8,128)S(1)}, f32[48,128]{1,0:T(8,128)S(1)}, u32[]{:S(2)}, u32[]{:S(2)}) collective-permute-start(f32[48,128]{1,0:T(8,128)S(1)} %fusion), channel_id=1, source_target_pairs={{0,8},{4,12},{8,0},{12,4},{1,9},{5,13},{9,1},{13,5},{2,10},{6,14},... | collective-permute-start | bytes 73736 | tf_op jit(solution)/shard_map/ppermute | solution.py:566
  30.3 6.2 %collective-permute-start.9 = (f32[48,128]{1,0:T(8,128)S(1)}, f32[48,128]{1,0:T(8,128)S(1)}, u32[]{:S(2)}, u32[]{:S(2)}) collective-permute-start(f32[48,128]{1,0:T(8,128)S(1)} %add.26), channel_id=1, source_target_pairs={{0,1},{1,0},{2,3},{3,2},{4,5},{5,4},{6,7},{7,6},{8,9},{9,8},{10,11... | collective-permute-start | bytes 73736 | tf_op jit(solution)/shard_map/ppermute | solution.py:566
  36.5 4.7 %collective-permute-start.10 = (f32[48,128]{1,0:T(8,128)S(1)}, f32[48,128]{1,0:T(8,128)S(1)}, u32[]{:S(2)}, u32[]{:S(2)}) collective-permute-start(f32[48,128]{1,0:T(8,128)S(1)} %add.27), channel_id=1, source_target_pairs={{0,2},{1,3},{2,0},{3,1},{4,6},{5,7},{6,4},{7,5},{8,10},{9,11},{10,... | collective-permute-start | bytes 73736 | tf_op jit(solution)/shard_map/ppermute | solution.py:566

commit v2 on v1

--- a/solution.py
+++ b/solution.py
@@ -11,7 +11,7 @@
 SLAB = 16
 NODE_ROWS = 112
 FORCE_ROWS = 192
-OTHER_TOP = 120
+OTHER_TOP = 60
 EDGE = 64
 
 
@@ -491,9 +491,15 @@
 
     both = lax.fori_loop(0, sx + 1, gram_layer, jnp.zeros((width, 2 * width), f32))
     gram_stiff = both[:, 0:width]
-    gram_out[...] = jnp.zeros(gram_out.shape, f32)
-    gram_out[:, 0:width] = gram_stiff
-    gram_out[:, 64 : 64 + width] = both[:, width : 2 * width]
+    one, two, three = cols, 2 * cols, 3 * cols
+    empty = jnp.zeros((cols, 64 - 5 * cols), f32)
+    first = []
+    second = []
+    for whole in (gram_stiff, both[:, width : 2 * width]):
+        first += [whole[0:one], whole[two:three, two:three], empty]
+        second += [whole[three:, three:], whole[one:two, one:], whole[two:three, three:], empty]
+    gram_out[0:cols] = jnp.concatenate(first, 1)
+    gram_out[cols : 2 * cols] = jnp.concatenate(second, 1)
 
 
 def finish_kernel(
@@ -508,18 +514,31 @@
     quotient = jnp.sum(top, 1, keepdims=True) / jnp.sum(bottom, 1, keepdims=True)
     quotient_row = jnp.sum(top, 0, keepdims=True) / jnp.sum(bottom, 0, keepdims=True)
     for at, out in ((0, stiff_gram), (64, mass_gram)):
-        whole = gram[:, at : at + 4 * cols]
-        rows = jnp.concatenate(
-            [whole[0:cols], whole[cols : 2 * cols] - quotient * whole[2 * cols : 3 * cols], whole[3 * cols :]], 0
+        first = gram[0:cols, at : at + 64]
+        second = gram[cols : 2 * cols, at : at + 64]
+        cc, ca, cb, cp, bb = [first[:, i * cols : (i + 1) * cols] for i in range(5)]
+        pp, aa, ab, ap, bp = [second[:, i * cols : (i + 1) * cols] for i in range(5)]
+        cross = ab * quotient_row
+        blank = jnp.zeros((cols, cols), f32)
+        tail = jnp.zeros((cols, sz - 3 * cols), f32)
+        above = jnp.concatenate(
+            [
+                jnp.concatenate([blank, ca - cb * quotient_row, cp, tail], 1),
+                jnp.concatenate([blank, -cross, ap - quotient * bp, tail], 1),
+                jnp.zeros((sz - 2 * cols, sz), f32),
+            ],
+            0,
         )
-        out[:, 0, :] = (1.0 / dof) * jnp.concatenate(
+        level = jnp.concatenate(
             [
-                rows[:, 0:cols],
-                rows[:, cols : 2 * cols] - quotient_row * rows[:, 2 * cols : 3 * cols],
-                rows[:, 3 * cols :],
+                jnp.concatenate([cc, blank, blank], 1),
+                jnp.concatenate([blank, aa + quotient * quotient_row * bb, blank], 1),
+                jnp.concatenate([blank, blank, pp], 1),
             ],
-            1,
+            0,
         )
+        full = level + (above + above.T)[0 : 3 * cols, 0 : 3 * cols]
+        out[:, 0, :] = (1.0 / dof) * full
 
     def weigh(value, total):
         squared = value * value
@@ -669,9 +688,9 @@
     _, gram = pl.pallas_call(
         lambda *refs: gram_kernel(sizes, *refs),
         in_specs=[vmem] * 7,
-        out_shape=(kept((sx + 1) * width * 3 * span, sz), kept(width, 128)),
+        out_shape=(kept((sx + 1) * width * 3 * span, sz), kept(2 * cols, 128)),
         input_output_aliases={6: 0},
-        compiler_params=pltpu.CompilerParams(vmem_limit_bytes=16 << 20),
+        compiler_params=low_limit,
         name="gram",
     )(*[near(x) for x in (basis, stiff, lumped, op_high, op_low, prev_parts, applied)])
     gram = jnp.concatenate([gram[0:16] + other[energies:], gram[16:]], 0)

time: 43.3 us -> 42.9 us (level)
  no operation moved by 1% of the time
where the time goes in v2:
time: 42.9 us; the launch traced here: 42.7 us
  starting transfers between devices  22 us (51%)
  Pallas kernels  12.9 us (30%)
  waiting for transfers between devices  6.87 us (16%)
  between operations  0.79 us (2%)
    ppermute x4, starting transfers between devices, sum_over(): lax.ppermute(value, axis, [(i, i ^ distance) for i in range(count)])  10.3 us
    ppermute x4, waiting for transfers between devices, sum_over(): lax.ppermute(value, axis, [(i, i ^ distance) for i in range(count)])  6.85 us
    pallas_call x1, Pallas kernels, shards(): pl.pallas_call(lambda *refs: gram_kernel(sizes, *refs), in_specs=[vmem] *...  3.83 us
    ppermute x1, starting transfers between devices, shards(): rows_a = lax.ppermute(message_a, 'by', pairs('by', 0))  3.11 us
    ppermute x1, starting transfers between devices, shards(): pair_a = lax.ppermute(own, 'bx', pairs('bx', 0))  2.92 us
    pallas_call x1, Pallas kernels, shards(): pl.pallas_call(lambda *refs: current_kernel(sizes, *refs), in_specs=[smem...  2.87 us
    ppermute x1, starting transfers between devices, shards(): corner_a = lax.ppermute(corner, 'bx', pairs('bx', 0))  2.06 us
    pallas_call x1, Pallas kernels, shards(): pl.pallas_call(lambda *refs: finish_kernel(sizes, dof, *refs), in_specs=[...  1.77 us
  transfers between devices with their start and end apart: 11, of which 4 were waited for; matrix products, arithmetic and copies ran while one was open for 0% of the time, Pallas kernels for 16%

profile of v2, /device:TPU:0, one launch (start us, length us, event | category | flops | bytes accessed | tf_op | source)
XLA Modules:
  0.0 42.7 jit_solution(15617767608275494654)
XLA Ops:
  0.6 1.3 %prepare.1 = (f32[944,128]{1,0:T(8,128)S(1)}, f32[576,128]{1,0:T(8,128)S(1)}, f32[232,128]{1,0:T(8,128)S(1)}, f32[232,128]{1,0:T(8,128)S(1)}) custom-call(s32[1]{0:T(128)} %bitcast.2.refs_0_, f32[1,12,3,2,8,128]{5,4,3,2,1,0:T(8,128)} %refs_1_.2, f32[1,12,3,2,8,128]{5,4,3,2,1,0:T(8,128)} %refs_2_.2, f32[2,8,128]{2,1,0:T(8,128)} %refs_3_.2, ...), custom_call_target="tpu_custom_call" | custom-call | tf_op jit(solution)/shard_map/prepare/pallas_call | solution.py:618
  1.9 3.1 %collective-permute-start.2 = (f32[232,128]{1,0:T(8,128)S(1)}, f32[232,128]{1,0:T(8,128)S(1)}, u32[]{:S(2)}, u32[]{:S(2)}) collective-permute-start(f32[232,128]{1,0:T(8,128)S(1)} %get-tuple-element.35), channel_id=1, source_target_pairs={{0,1},{1,0},{2,3},{3,2},{4,5},{5,4},{6,7},{7,6},{8,9},{9,8},{10,11... | collective-permute-start | bytes 356360 | tf_op jit(solution)/shard_map/ppermute | solution.py:626
  5.0 0.7 %collective-permute-start.3 = (f32[232,128]{1,0:T(8,128)S(1)}, f32[232,128]{1,0:T(8,128)S(1)}, u32[]{:S(2)}, u32[]{:S(2)}) collective-permute-start(f32[232,128]{1,0:T(8,128)S(1)} %get-tuple-element.36), channel_id=1, source_target_pairs={{1,2},{2,1},{5,6},{6,5},{9,10},{10,9},{13,14},{14,13},{17,18},{18,... | collective-permute-start | bytes 356360 | tf_op jit(solution)/shard_map/ppermute | solution.py:627
  5.7 0.7 %collective-permute-start.1 = (f32[944,128]{1,0:T(8,128)S(1)}, f32[944,128]{1,0:T(8,128)S(1)}, u32[]{:S(2)}, u32[]{:S(2)}) collective-permute-start(f32[944,128]{1,0:T(8,128)S(1)} %get-tuple-element.34.refs_0_), channel_id=1, source_target_pairs={{4,8},{8,4},{5,9},{9,5},{6,10},{10,6},{7,11},{11,7},{20,24},{24,20... | collective-permute-start | bytes 1449992 | tf_op jit(solution)/shard_map/ppermute | solution.py:641
  6.4 2.9 %collective-permute-start = (f32[944,128]{1,0:T(8,128)S(1)}, f32[944,128]{1,0:T(8,128)S(1)}, u32[]{:S(2)}, u32[]{:S(2)}) collective-permute-start(f32[944,128]{1,0:T(8,128)S(1)} %get-tuple-element.34.refs_0_), channel_id=1, source_target_pairs={{0,4},{4,0},{8,12},{12,8},{1,5},{5,1},{9,13},{13,9},{2,6},{6,2},{1... | collective-permute-start | bytes 1449992 | tf_op jit(solution)/shard_map/ppermute | solution.py:640
  9.4 0.7 %collective-permute-start.5 = (f32[312,128]{1,0:T(8,128)S(1)}, f32[312,128]{1,0:T(8,128)S(1)}, u32[]{:S(2)}, u32[]{:S(2)}) collective-permute-start(f32[312,128]{1,0:T(8,128)S(1)} %pad_maximum_fusion), channel_id=1, source_target_pairs={{4,8},{8,4},{5,9},{9,5},{6,10},{10,6},{7,11},{11,7},{20,24},{24,20... | collective-permute-start | bytes 479240 | tf_op jit(solution)/shard_map/ppermute | solution.py:644
  10.1 2.1 %collective-permute-start.4 = (f32[312,128]{1,0:T(8,128)S(1)}, f32[312,128]{1,0:T(8,128)S(1)}, u32[]{:S(2)}, u32[]{:S(2)}) collective-permute-start(f32[312,128]{1,0:T(8,128)S(1)} %pad_maximum_fusion), channel_id=1, source_target_pairs={{0,4},{4,0},{8,12},{12,8},{1,5},{5,1},{9,13},{13,9},{2,6},{6,2},{1... | collective-permute-start | bytes 479240 | tf_op jit(solution)/shard_map/ppermute | solution.py:643
  12.1 1.7 %operator.1 = (bf16[304,256]{1,0:T(8,128)(2,1)S(1)}, bf16[304,256]{1,0:T(8,128)(2,1)S(1)}) custom-call(f32[24,24]{1,0:T(8,128)} %refs_0_.1, bf16[2,304,24]{2,1,0:T(8,128)(2,1)} %constant.37.clone.refs_1_, bf16[24,256]{1,0:T(8,128)(2,1)} %constant.38.clone.refs_2_, bf16[2,304,256]{2,1,0:T(8,128)(2,1)} %constant.39.clone.refs_3_), custom_call_target="tpu_custom_call" | custom-call | tf_op jit(solution)/shard_map/operator/pallas_call | solution.py:632
  13.8 0.1 pad_add_fusion.refs_0_
  13.9 1.5 %early.1 = (f32[6480,128]{1,0:T(8,128)S(1)}, f32[960,128]{1,0:T(8,128)S(1)}, f32[32,128]{1,0:T(8,128)S(1)}, f32[64,128]{1,0:T(8,128)S(1)}, f32[64,128]{1,0:T(8,1...) custom-call(f32[944,128]{1,0:T(8,128)S(1)} %get-tuple-element.34.ref, ...), custom_call_target="tpu_custom_call" | custom-call | tf_op jit(solution)/shard_map/early/pallas_call | solution.py:663
  15.4 0.0 collective-permute-done.4.refs_3_
  15.4 0.0 collective-permute-done.1.refs_2_
  15.4 2.9 %current.1 = (f32[6480,128]{1,0:T(8,128)S(1)}, f32[960,128]{1,0:T(8,128)S(1)}, f32[32,128]{1,0:T(8,128)S(1)}, f32[64,128]{1,0:T(8,128)S(1)}, f32[64,128]{1,0:T(8...) custom-call(s32[2]{0:T(128)S(1)} %pad_add_fusion.refs_0_, ...), custom_call_target="tpu_custom_call", output_to_operand_aliasing={{0}: (8, {}), {1}: (9, {}), {2}: (10, {}), {3}: (11, {}), {... | custom-call | tf_op jit(solution)/shard_map/current/pallas_call | solution.py:670
  18.3 1.5 %collective-permute-start.6 = (f32[208,128]{1,0:T(8,128)S(1)}, f32[208,128]{1,0:T(8,128)S(1)}, u32[]{:S(2)}, u32[]{:S(2)}) collective-permute-start(f32[208,128]{1,0:T(8,128)S(1)} %get-tuple-element.55), channel_id=1, source_target_pairs={{0,16},{16,0},{1,17},{17,1},{2,18},{18,2},{3,19},{19,3},{4,20},{20... | collective-permute-start | bytes 319496 | tf_op jit(solution)/shard_map/ppermute | solution.py:687
  19.8 3.8 %gram.1 = (f32[3888,128]{1,0:T(8,128)S(1)}, f32[24,128]{1,0:T(8,128)S(1)}) custom-call(f32[6480,128]{1,0:T(8,128)S(1)} %get-tuple-element.49.refs_0_, f32[32,128]{1,0:T(8,128)S(1)} %get-tuple-element.50.refs_1_, f32[48,128]{1,0:T(8,128)S(1)} %get-tuple-element.51.refs_2_, ...), custom_call_target="tpu_custom_call", output_to_operand_aliasing={{0}: (6, {})} | custom-call | tf_op jit(solution)/shard_map/gram/pallas_call | solution.py:688
  23.7 1.8 %collective-permute-start.7 = (f32[24,128]{1,0:T(8,128)S(1)}, f32[24,128]{1,0:T(8,128)S(1)}, u32[]{:S(2)}, u32[]{:S(2)}) collective-permute-start(f32[24,128]{1,0:T(8,128)S(1)} %pad_maximum_fusion.1), channel_id=1, source_target_pairs={{0,4},{4,0},{8,12},{12,8},{1,5},{5,1},{9,13},{13,9},{2,6},{6,2},{1... | collective-permute-start | bytes 36872 | tf_op jit(solution)/shard_map/ppermute | solution.py:585
  25.4 0.8 %collective-permute-done.7 = f32[24,128]{1,0:T(8,128)S(1)} collective-permute-done((f32[24,128]{1,0:T(8,128)S(1)}, f32[24,128]{1,0:T(8,128)S(1)}, u32[]{:S(2)}, u32[]{:S(2)}) %collective-permute-start.7) | collective-permute-done | bytes 12320 | tf_op jit(solution)/shard_map/ppermute | solution.py:585
  26.3 2.2 %collective-permute-start.8 = (f32[24,128]{1,0:T(8,128)S(1)}, f32[24,128]{1,0:T(8,128)S(1)}, u32[]{:S(2)}, u32[]{:S(2)}) collective-permute-start(f32[24,128]{1,0:T(8,128)S(1)} %fusion), channel_id=1, source_target_pairs={{0,8},{4,12},{8,0},{12,4},{1,9},{5,13},{9,1},{13,5},{2,10},{6,14},... | collective-permute-start | bytes 36872 | tf_op jit(solution)/shard_map/ppermute | solution.py:585
  28.5 1.7 %collective-permute-done.8 = f32[24,128]{1,0:T(8,128)S(1)} collective-permute-done((f32[24,128]{1,0:T(8,128)S(1)}, f32[24,128]{1,0:T(8,128)S(1)}, u32[]{:S(2)}, u32[]{:S(2)}) %collective-permute-start.8) | collective-permute-done | bytes 12320 | tf_op jit(solution)/shard_map/ppermute | solution.py:585
  30.2 4.4 %collective-permute-start.9 = (f32[24,128]{1,0:T(8,128)S(1)}, f32[24,128]{1,0:T(8,128)S(1)}, u32[]{:S(2)}, u32[]{:S(2)}) collective-permute-start(f32[24,128]{1,0:T(8,128)S(1)} %add.26), channel_id=1, source_target_pairs={{0,1},{1,0},{2,3},{3,2},{4,5},{5,4},{6,7},{7,6},{8,9},{9,8},{10,11... | collective-permute-start | bytes 36872 | tf_op jit(solution)/shard_map/ppermute | solution.py:585
  34.6 1.7 %collective-permute-done.9 = f32[24,128]{1,0:T(8,128)S(1)} collective-permute-done((f32[24,128]{1,0:T(8,128)S(1)}, f32[24,128]{1,0:T(8,128)S(1)}, u32[]{:S(2)}, u32[]{:S(2)}) %collective-permute-start.9) | collective-permute-done | bytes 12320 | tf_op jit(solution)/shard_map/ppermute | solution.py:585
  36.3 1.9 %collective-permute-start.10 = (f32[24,128]{1,0:T(8,128)S(1)}, f32[24,128]{1,0:T(8,128)S(1)}, u32[]{:S(2)}, u32[]{:S(2)}) collective-permute-start(f32[24,128]{1,0:T(8,128)S(1)} %add.27), channel_id=1, source_target_pairs={{0,2},{1,3},{2,0},{3,1},{4,6},{5,7},{6,4},{7,5},{8,10},{9,11},{10,... | collective-permute-start | bytes 36872 | tf_op jit(solution)/shard_map/ppermute | solution.py:585
  38.2 2.7 %collective-permute-done.10 = f32[24,128]{1,0:T(8,128)S(1)} collective-permute-done((f32[24,128]{1,0:T(8,128)S(1)}, f32[24,128]{1,0:T(8,128)S(1)}, u32[]{:S(2)}, u32[]{:S(2)}) %collective-permute-start.10) | collective-permute-done | bytes 12320 | tf_op jit(solution)/shard_map/ppermute | solution.py:585
  40.9 1.8 %finish.1 = (f32[36,1,36]{2,1,0:T(1,128)}, f32[36,1,36]{2,1,0:T(1,128)}, f32[1,12,3,2,8,128]{5,4,3,2,1,0:T(8,128)}, f32[2,8,64]{2,1,0:T(8,128)}) custom-call(s32[2]{0:T(128)S(1)} %pad_add_fusion.refs_0_, f32[24,128]{1,0:T(8,128)S(1)} %add.28.refs_1_, f32[576,128]{1,0:T(8,128)S(1)} %get-tuple-element.56.refs_2_, f32[576,128]{1,0:T(8,128)S(1)} %get-tuple-element.57.refs_3_, ...), custom_call_target="tpu_custom_call" | custom-call | tf_op jit(solution)/shard_map/finish/pallas_call | solution.py:698
  (15 shorter events, 0.1 us)
Async XLA Ops:
  1.9 7.4 %collective-permute-start.2 = (f32[232,128]{1,0:T(8,128)S(1)}, f32[232,128]{1,0:T(8,128)S(1)}, u32[]{:S(2)}, u32[]{:S(2)}) collective-permute-start(f32[232,128]{1,0:T(8,128)S(1)} %get-tuple-element.35), channel_id=1, source_target_pairs={{0,1},{1,0},{2,3},{3,2},{4,5},{5,4},{6,7},{7,6},{8,9},{9,8},{10,11... | collective-permute-start | bytes 356360 | tf_op jit(solution)/shard_map/ppermute | solution.py:626
  5.0 4.3 %collective-permute-start.3 = (f32[232,128]{1,0:T(8,128)S(1)}, f32[232,128]{1,0:T(8,128)S(1)}, u32[]{:S(2)}, u32[]{:S(2)}) collective-permute-start(f32[232,128]{1,0:T(8,128)S(1)} %get-tuple-element.36), channel_id=1, source_target_pairs={{1,2},{2,1},{5,6},{6,5},{9,10},{10,9},{13,14},{14,13},{17,18},{18,... | collective-permute-start | bytes 356360 | tf_op jit(solution)/shard_map/ppermute | solution.py:627
  5.7 9.7 %collective-permute-start.1 = (f32[944,128]{1,0:T(8,128)S(1)}, f32[944,128]{1,0:T(8,128)S(1)}, u32[]{:S(2)}, u32[]{:S(2)}) collective-permute-start(f32[944,128]{1,0:T(8,128)S(1)} %get-tuple-element.34.refs_0_), channel_id=1, source_target_pairs={{4,8},{8,4},{5,9},{9,5},{6,10},{10,6},{7,11},{11,7},{20,24},{24,20... | collective-permute-start | bytes 1449992 | tf_op jit(solution)/shard_map/ppermute | solution.py:641
  6.4 9.0 %collective-permute-start = (f32[944,128]{1,0:T(8,128)S(1)}, f32[944,128]{1,0:T(8,128)S(1)}, u32[]{:S(2)}, u32[]{:S(2)}) collective-permute-start(f32[944,128]{1,0:T(8,128)S(1)} %get-tuple-element.34.refs_0_), channel_id=1, source_target_pairs={{0,4},{4,0},{8,12},{12,8},{1,5},{5,1},{9,13},{13,9},{2,6},{6,2},{1... | collective-permute-start | bytes 1449992 | tf_op jit(solution)/shard_map/ppermute | solution.py:640
  9.4 6.0 %collective-permute-start.5 = (f32[312,128]{1,0:T(8,128)S(1)}, f32[312,128]{1,0:T(8,128)S(1)}, u32[]{:S(2)}, u32[]{:S(2)}) collective-permute-start(f32[312,128]{1,0:T(8,128)S(1)} %pad_maximum_fusion), channel_id=1, source_target_pairs={{4,8},{8,4},{5,9},{9,5},{6,10},{10,6},{7,11},{11,7},{20,24},{24,20... | collective-permute-start | bytes 479240 | tf_op jit(solution)/shard_map/ppermute | solution.py:644
  10.1 5.3 %collective-permute-start.4 = (f32[312,128]{1,0:T(8,128)S(1)}, f32[312,128]{1,0:T(8,128)S(1)}, u32[]{:S(2)}, u32[]{:S(2)}) collective-permute-start(f32[312,128]{1,0:T(8,128)S(1)} %pad_maximum_fusion), channel_id=1, source_target_pairs={{0,4},{4,0},{8,12},{12,8},{1,5},{5,1},{9,13},{13,9},{2,6},{6,2},{1... | collective-permute-start | bytes 479240 | tf_op jit(solution)/shard_map/ppermute | solution.py:643
  18.3 5.4 %collective-permute-start.6 = (f32[208,128]{1,0:T(8,128)S(1)}, f32[208,128]{1,0:T(8,128)S(1)}, u32[]{:S(2)}, u32[]{:S(2)}) collective-permute-start(f32[208,128]{1,0:T(8,128)S(1)} %get-tuple-element.55), channel_id=1, source_target_pairs={{0,16},{16,0},{1,17},{17,1},{2,18},{18,2},{3,19},{19,3},{4,20},{20... | collective-permute-start | bytes 319496 | tf_op jit(solution)/shard_map/ppermute | solution.py:687
  23.7 2.6 %collective-permute-start.7 = (f32[24,128]{1,0:T(8,128)S(1)}, f32[24,128]{1,0:T(8,128)S(1)}, u32[]{:S(2)}, u32[]{:S(2)}) collective-permute-start(f32[24,128]{1,0:T(8,128)S(1)} %pad_maximum_fusion.1), channel_id=1, source_target_pairs={{0,4},{4,0},{8,12},{12,8},{1,5},{5,1},{9,13},{13,9},{2,6},{6,2},{1... | collective-permute-start | bytes 36872 | tf_op jit(solution)/shard_map/ppermute | solution.py:585
  26.3 3.9 %collective-permute-start.8 = (f32[24,128]{1,0:T(8,128)S(1)}, f32[24,128]{1,0:T(8,128)S(1)}, u32[]{:S(2)}, u32[]{:S(2)}) collective-permute-start(f32[24,128]{1,0:T(8,128)S(1)} %fusion), channel_id=1, source_target_pairs={{0,8},{4,12},{8,0},{12,4},{1,9},{5,13},{9,1},{13,5},{2,10},{6,14},... | collective-permute-start | bytes 36872 | tf_op jit(solution)/shard_map/ppermute | solution.py:585
  30.2 6.1 %collective-permute-start.9 = (f32[24,128]{1,0:T(8,128)S(1)}, f32[24,128]{1,0:T(8,128)S(1)}, u32[]{:S(2)}, u32[]{:S(2)}) collective-permute-start(f32[24,128]{1,0:T(8,128)S(1)} %add.26), channel_id=1, source_target_pairs={{0,1},{1,0},{2,3},{3,2},{4,5},{5,4},{6,7},{7,6},{8,9},{9,8},{10,11... | collective-permute-start | bytes 36872 | tf_op jit(solution)/shard_map/ppermute | solution.py:585
  36.3 4.6 %collective-permute-start.10 = (f32[24,128]{1,0:T(8,128)S(1)}, f32[24,128]{1,0:T(8,128)S(1)}, u32[]{:S(2)}, u32[]{:S(2)}) collective-permute-start(f32[24,128]{1,0:T(8,128)S(1)} %add.27), channel_id=1, source_target_pairs={{0,2},{1,3},{2,0},{3,1},{4,6},{5,7},{6,4},{7,5},{8,10},{9,11},{10,... | collective-permute-start | bytes 36872 | tf_op jit(solution)/shard_map/ppermute | solution.py:585
